TPU v7x, 32 devices: a whole 2x2x4 slice. The times are simulated.
32 devices in a mesh: tm: 16 (over z, y, core), video: 2 (over x).
Axes of the slice: x: 2, y: 2, z: 4, core: 2. Of those that a mesh axis runs over, the one named last changes fastest.
Arguments:
- memory: bfloat16 [2, 16, 1, 64, 768], P('video', 'tm'), may hold values from -24 to 24
- frames: float32 [2, 16, 1, 128, 768], P('video', 'tm'), may hold values from -6 to 6
- mem_cot: bfloat16 [2, 16, 1, 64, 768], P('video', 'tm'), may hold values from -3 to 3
- slot_used: int32 [2, 16, 1], P('video', 'tm'), may hold values 0 or 1
- key_bias: float32 [2, 16, 1, 12, 128], P('video', 'tm'), may hold values from -6 to 300
- start_offset: int32 [2, 1], P('video'), may hold values from 0 to 2047
- norm_gain: float32 [768], replicated, may hold values from 0.5 to 1.5
- w_query: bfloat16 [768, 768], replicated, may hold values from -0.21875 to 0.21875
- w_key: bfloat16 [768, 768], replicated, may hold values from -0.21875 to 0.21875
- w_value: bfloat16 [768, 768], replicated, may hold values from -0.21875 to 0.21875
- w_out: bfloat16 [768, 768], replicated, may hold values from -0.21875 to 0.21875
Outputs:
- grad_memory: float32 [2, 16, 1, 64, 768], P('video', 'tm')
- grad_query: float32 [768, 768], P('tm', 'video')
- grad_key: float32 [768, 768], P('tm', 'video')
- grad_value: float32 [768, 768], P('tm', 'video')
- grad_out: float32 [768, 768], P('tm', 'video')
- grad_gain: float32 [768], replicated
All inputs are finite; a program needn't handle non-finite values. No bound on the sum of `slot_used` on one device may be relied on, other than what follows from the above.
Results may differ from a plain program's by a relative error of at most 0.019.
Values sent between devices are 32-bit elements; how exact they have to be, the bound alone decides.
A program may use at most 64 MiB of HBM per device.

v0:
```python
import math

import jax
import jax.numpy as jnp
from jax import lax
from jax.sharding import PartitionSpec as P

H = 12
HD = 64


NORM_EPSILON = 1e-06


def from_behind(value, axis, steps):
    count = lax.axis_size(axis)
    initial, last = (max(0, -steps), min(count, count - steps))
    return lax.ppermute(value, axis, [(source, source + steps) for source in range(initial, last)])


def product(form, left, right):
    return jnp.einsum(form, left, right, preferred_element_type=jnp.float32)


def encoding(offsets, position, clip_len, features):
    within = jnp.arange(clip_len, dtype=jnp.int32)
    frame_time = offsets[:, None] + position * clip_len + within[None, :]
    half_width = features // 2
    frequency = 0.0625 * jnp.exp(
        -math.log(1000.0) * jnp.arange(half_width, dtype=jnp.float32) / half_width
    )
    phases = frame_time.astype(jnp.float32)[:, :, None] * frequency
    return jnp.concatenate([jnp.sin(phases), jnp.cos(phases)], axis=-1)


def recompute(
    memory_full, frame_rows, bias_rows, offsets, position, norm_gain, w_query, w_key, w_value
):
    batch, row_count, features = memory_full.shape
    inv_rms = lax.rsqrt(jnp.mean(memory_full * memory_full, axis=-1, keepdims=True) + NORM_EPSILON)
    unit_rows = memory_full * inv_rms
    normed = (unit_rows * norm_gain).astype(jnp.bfloat16)
    key_input = (frame_rows + encoding(offsets, position, frame_rows.shape[1], features)).astype(
        jnp.bfloat16
    )
    query_proj = product("brd,de->bre", normed, w_query).astype(jnp.bfloat16)
    key_proj = product("bld,de->ble", key_input, w_key).astype(jnp.bfloat16)
    value_proj = product("bld,de->ble", key_input, w_value).astype(jnp.bfloat16)
    query_heads = query_proj.reshape(batch, row_count, H, HD)
    key_heads = key_proj.reshape(batch, -1, H, HD)
    value_heads = value_proj.reshape(batch, -1, H, HD)
    scores = (
        product("brhd,blhd->bhrl", query_heads, key_heads) * HD ** (-0.5) + bias_rows[:, :, None, :]
    )
    row_max = jnp.max(scores, axis=-1, keepdims=True)
    exp_scores = jnp.exp(scores - row_max)
    attn_prob = exp_scores / jnp.sum(exp_scores, axis=-1, keepdims=True)
    attn_half = attn_prob.astype(jnp.bfloat16)
    attended = (
        product("bhrl,blhd->brhd", attn_half, value_heads)
        .astype(jnp.bfloat16)
        .reshape(batch, row_count, features)
    )
    return (
        inv_rms,
        unit_rows,
        normed,
        key_input,
        query_heads,
        key_heads,
        value_heads,
        attn_prob,
        attn_half,
        attended,
    )


def chain_part(
    grad_in,
    slot_live,
    unit_rows,
    inv_rms,
    attn_prob,
    key_heads,
    value_heads,
    norm_gain,
    w_query,
    w_out,
):
    batch, row_count, features = grad_in.shape
    out_grad = (slot_live[:, None, None] * grad_in).astype(jnp.bfloat16)
    att_grad = product("bre,de->brd", out_grad, w_out).astype(jnp.bfloat16)
    att_heads = att_grad.reshape(batch, row_count, H, HD)
    prob_grad = product("brhd,blhd->bhrl", att_heads, value_heads)
    inner_sum = jnp.sum(attn_prob * prob_grad, axis=-1, keepdims=True)
    score_grad = (attn_prob * (prob_grad - inner_sum) * HD ** (-0.5)).astype(jnp.bfloat16)
    query_grad = (
        product("bhrl,blhd->brhd", score_grad, key_heads)
        .astype(jnp.bfloat16)
        .reshape(batch, row_count, features)
    )
    normed_grad = product("bre,de->brd", query_grad, w_query)
    gain_term = jnp.sum(normed_grad * unit_rows, axis=(0, 1))
    scaled_grad = normed_grad * norm_gain
    passed = grad_in + inv_rms * (
        scaled_grad - unit_rows * jnp.mean(scaled_grad * unit_rows, axis=-1, keepdims=True)
    )
    return (passed, out_grad, att_heads, score_grad, query_grad, gain_term)


def weight_part(
    normed, key_input, query_heads, attn_half, attended, out_grad, att_heads, score_grad, query_grad
):
    batch, length, features = key_input.shape
    value_grad = (
        product("bhrl,brhd->blhd", attn_half, att_heads)
        .astype(jnp.bfloat16)
        .reshape(batch, length, features)
    )
    key_grad = (
        product("bhrl,brhd->blhd", score_grad, query_heads)
        .astype(jnp.bfloat16)
        .reshape(batch, length, features)
    )
    return (
        product("brd,bre->de", normed, query_grad),
        product("bld,ble->de", key_input, key_grad),
        product("bld,ble->de", key_input, value_grad),
        product("brd,bre->de", attended, out_grad),
    )


def run_chain(clip_work, inner_state, chain_rank, turn_count, stream_count, grad_shape):

    def pass_turn(carried, stream_pick, incoming):
        return (carried, jnp.zeros(grad_shape, jnp.float32))

    def one_turn(turn_index, carried):
        incoming, inner = carried
        stream_pick = turn_index - chain_rank
        active = jnp.logical_and(stream_pick >= 0, stream_pick < stream_count)
        stream_pick = jnp.clip(stream_pick, 0, stream_count - 1)
        inner, sending = lax.cond(active, clip_work, pass_turn, inner, stream_pick, incoming)
        received = from_behind(sending, "tm", -1)
        return (received, inner)

    start = (jnp.zeros(grad_shape, jnp.float32), inner_state)
    return lax.fori_loop(0, turn_count, one_turn, start)[1]


def put_row(stash, value, stream_pick):
    return lax.dynamic_update_index_in_dim(stash, value[0], stream_pick, 0)


def on_device(
    memory,
    frames,
    mem_cot,
    slot_used,
    key_bias,
    start_offset,
    norm_gain,
    w_query,
    w_key,
    w_value,
    w_out,
):
    owners = lax.axis_size("tm")
    groups = lax.axis_size("video")
    position = lax.axis_index("tm")
    memory_full = memory[0, 0].astype(jnp.float32)
    frame_rows = frames[0, 0]
    cotangent = mem_cot[0, 0].astype(jnp.float32)
    slot_live = slot_used[0, 0].astype(jnp.float32)
    bias_rows = key_bias[0, 0]
    offsets = start_offset[0]
    streams, row_count, features = memory_full.shape
    length = frame_rows.shape[1]
    heads = bias_rows.shape[1]
    chain_rank = owners - 1 - position
    turn_count = owners + streams - 1
    grad_shape = (row_count, features)
    row_half = jnp.zeros((streams, row_count, features), jnp.bfloat16)
    head_half = jnp.zeros((streams, row_count, heads, features // heads), jnp.bfloat16)
    prob_half = jnp.zeros((streams, heads, row_count, length), jnp.bfloat16)
    parts = recompute(
        memory_full, frame_rows, bias_rows, offsets, position, norm_gain, w_query, w_key, w_value
    )
    (
        inv_rms,
        unit_rows,
        normed,
        key_input,
        query_heads,
        key_heads,
        value_heads,
        attn_prob,
        attn_half,
        attended,
    ) = parts

    def clip_work(carried, stream_pick, incoming):
        memory_grads, out_stash, att_stash, score_stash, query_stash, sum_gain = carried

        def take_one(array):
            return lax.dynamic_index_in_dim(array, stream_pick, 0, keepdims=True)

        grad_in = incoming[None] + take_one(cotangent)
        passed, out_grad, att_heads, score_grad, query_grad, gain_term = chain_part(
            grad_in,
            take_one(slot_live),
            take_one(unit_rows),
            take_one(inv_rms),
            take_one(attn_prob),
            take_one(key_heads),
            take_one(value_heads),
            norm_gain,
            w_query,
            w_out,
        )
        return (
            (
                put_row(memory_grads, passed, stream_pick),
                put_row(out_stash, out_grad, stream_pick),
                put_row(att_stash, att_heads, stream_pick),
                put_row(score_stash, score_grad, stream_pick),
                put_row(query_stash, query_grad, stream_pick),
                sum_gain + gain_term,
            ),
            passed[0],
        )

    inner_state = (
        jnp.zeros_like(memory_full),
        row_half,
        head_half,
        prob_half,
        row_half,
        jnp.zeros((features,), jnp.float32),
    )
    final = run_chain(clip_work, inner_state, chain_rank, turn_count, streams, grad_shape)
    memory_grads, out_stash, att_stash, score_stash, query_stash, sum_gain = final
    sum_query, sum_key, sum_value, sum_out = weight_part(
        normed,
        key_input,
        query_heads,
        attn_half,
        attended,
        out_stash,
        att_stash,
        score_stash,
        query_stash,
    )
    gain_sum = lax.psum(sum_gain, ("tm", "video"))
    column_part = (
        lax.psum_scatter(sum_query, "video", scatter_dimension=1, tiled=True),
        lax.psum_scatter(sum_key, "video", scatter_dimension=1, tiled=True),
        lax.psum_scatter(sum_value, "video", scatter_dimension=1, tiled=True),
        lax.psum_scatter(sum_out, "video", scatter_dimension=1, tiled=True),
    )
    summed = (
        lax.psum_scatter(column_part[0], "tm", scatter_dimension=0, tiled=True),
        lax.psum_scatter(column_part[1], "tm", scatter_dimension=0, tiled=True),
        lax.psum_scatter(column_part[2], "tm", scatter_dimension=0, tiled=True),
        lax.psum_scatter(column_part[3], "tm", scatter_dimension=0, tiled=True),
    )
    mean_scale = 1.0 / (owners * groups * streams)
    return (
        memory_grads[None, None],
        summed[0] * mean_scale,
        summed[1] * mean_scale,
        summed[2] * mean_scale,
        summed[3] * mean_scale,
        gain_sum * mean_scale,
    )


def solution(mesh):
    return jax.shard_map(
        on_device,
        mesh=mesh,
        in_specs=(
            P("video", "tm", None, None, None),
            P("video", "tm", None, None, None),
            P("video", "tm", None, None, None),
            P("video", "tm", None),
            P("video", "tm", None, None, None),
            P("video", None),
            P(),
            P(),
            P(),
            P(),
            P(),
        ),
        out_specs=(
            P("video", "tm", None, None, None),
            P("tm", "video"),
            P("tm", "video"),
            P("tm", "video"),
            P("tm", "video"),
            P(),
        ),
        check_vma=False,
    )
```

profile of v0, /device:TPU:0, one launch (start us, length us, event | category | flops | bytes accessed | tf_op | source)
XLA Modules:
  0.0 664.5 jit_solution(14296088450288289299)
XLA Ops:
  8.7 1.0 fusion.22
  10.9 1.0 fusion.20
  11.9 1.8 convolution_convert_fusion.7
  16.0 1.0 convolution_convert_fusion.6
  17.0 1.1 copy.28
  18.4 2.1 fusion.47
  20.7 3.3 convolution_convert_fusion.2
  26.8 239.1 %while.25 = (s32[]{:T(128)}, f32[64,768]{1,0:T(8,128)S(1)}, f32[1,64,768]{2,1,0:T(8,128)}, bf16[1,64,768]{2,1,0:T(8,128)(2,1)}, bf16[1,64,12,64]{3,2,1,0:T(8,128...) while((s32[]{:T(128)}, f32[64,768]{1,0:T(8,128)S(1)}, ...), condition=%wide.region_9.10_spmd, body=%wide.region_3.9_spmd.sunk | while | flops 177536256 | bytes 14378907 | solution.py:148
  27.5 1.3 collective-permute-start
  28.8 2.2 collective-permute-done
  31.7 1.3 collective-permute-start
  33.0 6.8 %collective-permute-done = f32[64,768]{1,0:T(8,128)S(1)} collective-permute-done((f32[64,768]{1,0:T(8,128)}, f32[64,768]{1,0:T(8,128)S(1)}, u32[]{:S(2)}, u32[]{:S(2)}) %collective-permute-start) | collective-permute-done | bytes 196640 | tf_op jit(solution)/shard_map/while/body/eval_jaxpr/ppermute | solution.py:18
  40.5 1.3 collective-permute-start
  41.8 5.9 collective-permute-done
  48.3 1.3 collective-permute-start
  49.6 5.9 collective-permute-done
  56.2 1.3 collective-permute-start
  57.5 5.9 collective-permute-done
  64.1 1.3 collective-permute-start
  65.4 5.9 collective-permute-done
  71.9 1.3 collective-permute-start
  73.2 5.9 collective-permute-done
  79.8 1.3 collective-permute-start
  81.1 6.1 collective-permute-done
  87.9 1.3 collective-permute-start
  89.2 6.8 %collective-permute-done = f32[64,768]{1,0:T(8,128)S(1)} collective-permute-done((f32[64,768]{1,0:T(8,128)}, f32[64,768]{1,0:T(8,128)S(1)}, u32[]{:S(2)}, u32[]{:S(2)}) %collective-permute-start) | collective-permute-done | bytes 196640 | tf_op jit(solution)/shard_map/while/body/eval_jaxpr/ppermute | solution.py:18
  96.6 1.3 collective-permute-start
  97.9 6.8 %collective-permute-done = f32[64,768]{1,0:T(8,128)S(1)} collective-permute-done((f32[64,768]{1,0:T(8,128)}, f32[64,768]{1,0:T(8,128)S(1)}, u32[]{:S(2)}, u32[]{:S(2)}) %collective-permute-start) | collective-permute-done | bytes 196640 | tf_op jit(solution)/shard_map/while/body/eval_jaxpr/ppermute | solution.py:18
  105.4 1.3 collective-permute-start
  106.7 6.8 %collective-permute-done = f32[64,768]{1,0:T(8,128)S(1)} collective-permute-done((f32[64,768]{1,0:T(8,128)}, f32[64,768]{1,0:T(8,128)S(1)}, u32[]{:S(2)}, u32[]{:S(2)}) %collective-permute-start) | collective-permute-done | bytes 196640 | tf_op jit(solution)/shard_map/while/body/eval_jaxpr/ppermute | solution.py:18
  114.2 1.3 collective-permute-start
  115.5 6.8 %collective-permute-done = f32[64,768]{1,0:T(8,128)S(1)} collective-permute-done((f32[64,768]{1,0:T(8,128)}, f32[64,768]{1,0:T(8,128)S(1)}, u32[]{:S(2)}, u32[]{:S(2)}) %collective-permute-start) | collective-permute-done | bytes 196640 | tf_op jit(solution)/shard_map/while/body/eval_jaxpr/ppermute | solution.py:18
  122.9 1.3 collective-permute-start
  124.2 6.8 %collective-permute-done = f32[64,768]{1,0:T(8,128)S(1)} collective-permute-done((f32[64,768]{1,0:T(8,128)}, f32[64,768]{1,0:T(8,128)S(1)}, u32[]{:S(2)}, u32[]{:S(2)}) %collective-permute-start) | collective-permute-done | bytes 196640 | tf_op jit(solution)/shard_map/while/body/eval_jaxpr/ppermute | solution.py:18
  131.7 1.3 collective-permute-start
  133.0 6.8 %collective-permute-done = f32[64,768]{1,0:T(8,128)S(1)} collective-permute-done((f32[64,768]{1,0:T(8,128)}, f32[64,768]{1,0:T(8,128)S(1)}, u32[]{:S(2)}, u32[]{:S(2)}) %collective-permute-start) | collective-permute-done | bytes 196640 | tf_op jit(solution)/shard_map/while/body/eval_jaxpr/ppermute | solution.py:18
  140.5 1.3 collective-permute-start
  141.8 110.5 %collective-permute-done = f32[64,768]{1,0:T(8,128)S(1)} collective-permute-done((f32[64,768]{1,0:T(8,128)}, f32[64,768]{1,0:T(8,128)S(1)}, u32[]{:S(2)}, u32[]{:S(2)}) %collective-permute-start) | collective-permute-done | bytes 196640 | tf_op jit(solution)/shard_map/while/body/eval_jaxpr/ppermute | solution.py:18
  252.3 10.1 %conditional.2 = (f32[1,64,768]{2,1,0:T(8,128)}, bf16[1,64,768]{2,1,0:T(8,128)(2,1)}, bf16[1,64,12,64]{3,2,1,0:T(8,128)(2,1)}, bf16[1,12,64,128]{3,2,1,0:T(8,128...) conditional(s32[]{:T(128)} %convert_element_type.245, ...), branch_computations={%region_4.4_spmd, %region_5.8_spmd} | conditional | flops 177536256 | bytes 13592064 | solution.py:143
  253.0 1.8 convolution_convert_fusion.1
  254.8 0.9 broadcast_in_dim.19
  255.7 0.9 reshape.446
  256.5 1.4 fusion.3
  262.3 1.3 collective-permute-start
  263.6 2.2 collective-permute-done
  265.9 2.9 fusion.37
  270.2 2.6 convolution_convert_fusion.3
  272.9 1.9 fusion.49
  274.9 0.9 copy-done.12
  275.9 1.9 fusion.48
  278.8 2.0 fusion.34
  280.9 20.1 %reduce-scatter.21.cloned.1.call-done = f32[768,384]{1,0:T(8,128)} async-done(((f32[768,768]{1,0:T(8,128)}), f32[768,384]{1,0:T(8,128)}) %reduce-scatter.21.cloned.1.call-update) | async-done | bytes 1179664 | tf_op jit(solution)/shard_map/reduce_scatter | solution.py:259
  301.0 37.0 %reduce-scatter.17.cloned.1.call-done = f32[768,384]{1,0:T(8,128)} async-done(((f32[768,768]{1,0:T(8,128)}), f32[768,384]{1,0:T(8,128)}) %reduce-scatter.17.cloned.1.call-update) | async-done | bytes 1179664 | tf_op jit(solution)/shard_map/reduce_scatter | solution.py:258
  338.1 37.0 %reduce-scatter.13.cloned.1.call-done = f32[768,384]{1,0:T(8,128)} async-done(((f32[768,768]{1,0:T(8,128)}), f32[768,384]{1,0:T(8,128)}) %reduce-scatter.13.cloned.1.call-update) | async-done | bytes 1179664 | tf_op jit(solution)/shard_map/reduce_scatter | solution.py:257
  375.2 36.9 %reduce-scatter.9.cloned.1.call-done = f32[768,384]{1,0:T(8,128)} async-done(((f32[768,768]{1,0:T(8,128)}), f32[768,384]{1,0:T(8,128)}) %reduce-scatter.9.cloned.1.call-update) | async-done | bytes 1179664 | tf_op jit(solution)/shard_map/reduce_scatter | solution.py:256
  412.1 39.5 %psum.7 = f32[768]{0:T(1024)S(1)} all-reduce(f32[768]{0:T(1024)S(1)} %get-tuple-element.423), channel_id=1, replica_groups=mesh['tm'=16,'video'=2] {'tm','video'}, use_global_device_ids=true, to_apply=%region_18.19 | all-reduce | flops 768 | bytes 6144 | tf_op jit(solution)/shard_map/psum | solution.py:254
  452.1 21.7 %reduce-scatter.23.cloned.1.call-done = f32[48,384]{1,0:T(8,128)} async-done(((f32[768,384]{1,0:T(8,128)}), f32[48,384]{1,0:T(8,128)}) %reduce-scatter.23.cloned.1.call-update) | async-done | bytes 73744 | tf_op jit(solution)/shard_map/reduce_scatter | solution.py:265
  473.8 1.5 broadcast_multiply_fusion.1
  475.3 59.2 %reduce-scatter.19.cloned.1.call-done = f32[48,384]{1,0:T(8,128)} async-done(((f32[768,384]{1,0:T(8,128)}), f32[48,384]{1,0:T(8,128)}) %reduce-scatter.19.cloned.1.call-update) | async-done | bytes 73744 | tf_op jit(solution)/shard_map/reduce_scatter | solution.py:264
  534.5 1.5 broadcast_multiply_fusion.2
  536.0 59.3 %reduce-scatter.15.cloned.1.call-done = f32[48,384]{1,0:T(8,128)} async-done(((f32[768,384]{1,0:T(8,128)}), f32[48,384]{1,0:T(8,128)}) %reduce-scatter.15.cloned.1.call-update) | async-done | bytes 73744 | tf_op jit(solution)/shard_map/reduce_scatter | solution.py:263
  595.3 1.5 broadcast_multiply_fusion.3
  596.8 59.3 %reduce-scatter.11.cloned.1.call-done = f32[48,384]{1,0:T(8,128)} async-done(((f32[768,384]{1,0:T(8,128)}), f32[48,384]{1,0:T(8,128)}) %reduce-scatter.11.cloned.1.call-update) | async-done | bytes 73744 | tf_op jit(solution)/shard_map/reduce_scatter | solution.py:262
  656.2 1.5 broadcast_multiply_fusion.4
  (135 shorter events, 35.7 us)
Async XLA Ops:
  7.2 7.6 %copy-start = (bf16[768,768]{1,0:T(8,128)(2,1)S(1)}, bf16[768,768]{1,0:T(8,128)(2,1)}, u32[]{:S(2)}) copy-start(bf16[768,768]{1,0:T(8,128)(2,1)} %param.23) | copy-start | bytes 3538948
  7.2 6.7 %copy-start.21 = (bf16[1,1,1,64,768]{4,3,2,1,0:T(8,128)(2,1)S(1)}, bf16[1,1,1,64,768]{4,3,2,1,0:T(8,128)(2,1)}, u32[]{:S(2)}) copy-start(bf16[1,1,1,64,768]{4,3,2,1,0:T(8,128)(2,1)} %param.17) | copy-start | bytes 294916
  7.2 293.8 %reduce-scatter.21.cloned.1.call-start = ((), (), s32[]{:S(2)}) async-start(), calls=%async_computation.14 | async-start | bytes 3538944 | tf_op jit(solution)/shard_map/reduce_scatter | solution.py:259
  7.3 6.6 copy-start.22
  8.7 5.2 copy-start.26
  10.2 3.5 copy-start.24
  11.9 2.8 copy-start.15
  13.9 4.3 copy-start.11
  14.8 1.3 copy-start.17
  16.0 2.4 copy-start.4
  18.1 7.9 %copy-start.8 = (bf16[128,768]{0,1:T(8,128)(2,1)}, bf16[128,768]{0,1:T(8,128)(2,1)S(1)}, u32[]{:S(2)}) copy-start(bf16[128,768]{0,1:T(8,128)(2,1)S(1)} %copy.28) | copy-start | bytes 589828
  18.4 2.3 copy-start.14
  20.7 6.1 copy-start.1
  20.7 6.1 copy-start.18
  27.5 3.5 collective-permute-start
  31.7 8.1 %collective-permute-start = (f32[64,768]{1,0:T(8,128)}, f32[64,768]{1,0:T(8,128)S(1)}, u32[]{:S(2)}, u32[]{:S(2)}) collective-permute-start(f32[64,768]{1,0:T(8,128)} %get-tuple-element.616), channel_id=1, source_target_pairs={{2,0},{4,2},{6,4},{8,6},{10,8},{12,10},{14,12},{16,14},{18,16},{20... | collective-permute-start | bytes 589832 | tf_op jit(solution)/shard_map/while/body/eval_jaxpr/ppermute | solution.py:18
  40.5 7.2 %collective-permute-start = (f32[64,768]{1,0:T(8,128)}, f32[64,768]{1,0:T(8,128)S(1)}, u32[]{:S(2)}, u32[]{:S(2)}) collective-permute-start(f32[64,768]{1,0:T(8,128)} %get-tuple-element.616), channel_id=1, source_target_pairs={{2,0},{4,2},{6,4},{8,6},{10,8},{12,10},{14,12},{16,14},{18,16},{20... | collective-permute-start | bytes 589832 | tf_op jit(solution)/shard_map/while/body/eval_jaxpr/ppermute | solution.py:18
  48.3 7.2 %collective-permute-start = (f32[64,768]{1,0:T(8,128)}, f32[64,768]{1,0:T(8,128)S(1)}, u32[]{:S(2)}, u32[]{:S(2)}) collective-permute-start(f32[64,768]{1,0:T(8,128)} %get-tuple-element.616), channel_id=1, source_target_pairs={{2,0},{4,2},{6,4},{8,6},{10,8},{12,10},{14,12},{16,14},{18,16},{20... | collective-permute-start | bytes 589832 | tf_op jit(solution)/shard_map/while/body/eval_jaxpr/ppermute | solution.py:18
  56.2 7.2 %collective-permute-start = (f32[64,768]{1,0:T(8,128)}, f32[64,768]{1,0:T(8,128)S(1)}, u32[]{:S(2)}, u32[]{:S(2)}) collective-permute-start(f32[64,768]{1,0:T(8,128)} %get-tuple-element.616), channel_id=1, source_target_pairs={{2,0},{4,2},{6,4},{8,6},{10,8},{12,10},{14,12},{16,14},{18,16},{20... | collective-permute-start | bytes 589832 | tf_op jit(solution)/shard_map/while/body/eval_jaxpr/ppermute | solution.py:18
  64.1 7.2 %collective-permute-start = (f32[64,768]{1,0:T(8,128)}, f32[64,768]{1,0:T(8,128)S(1)}, u32[]{:S(2)}, u32[]{:S(2)}) collective-permute-start(f32[64,768]{1,0:T(8,128)} %get-tuple-element.616), channel_id=1, source_target_pairs={{2,0},{4,2},{6,4},{8,6},{10,8},{12,10},{14,12},{16,14},{18,16},{20... | collective-permute-start | bytes 589832 | tf_op jit(solution)/shard_map/while/body/eval_jaxpr/ppermute | solution.py:18
  71.9 7.2 %collective-permute-start = (f32[64,768]{1,0:T(8,128)}, f32[64,768]{1,0:T(8,128)S(1)}, u32[]{:S(2)}, u32[]{:S(2)}) collective-permute-start(f32[64,768]{1,0:T(8,128)} %get-tuple-element.616), channel_id=1, source_target_pairs={{2,0},{4,2},{6,4},{8,6},{10,8},{12,10},{14,12},{16,14},{18,16},{20... | collective-permute-start | bytes 589832 | tf_op jit(solution)/shard_map/while/body/eval_jaxpr/ppermute | solution.py:18
  79.8 7.4 %collective-permute-start = (f32[64,768]{1,0:T(8,128)}, f32[64,768]{1,0:T(8,128)S(1)}, u32[]{:S(2)}, u32[]{:S(2)}) collective-permute-start(f32[64,768]{1,0:T(8,128)} %get-tuple-element.616), channel_id=1, source_target_pairs={{2,0},{4,2},{6,4},{8,6},{10,8},{12,10},{14,12},{16,14},{18,16},{20... | collective-permute-start | bytes 589832 | tf_op jit(solution)/shard_map/while/body/eval_jaxpr/ppermute | solution.py:18
  87.9 8.1 %collective-permute-start = (f32[64,768]{1,0:T(8,128)}, f32[64,768]{1,0:T(8,128)S(1)}, u32[]{:S(2)}, u32[]{:S(2)}) collective-permute-start(f32[64,768]{1,0:T(8,128)} %get-tuple-element.616), channel_id=1, source_target_pairs={{2,0},{4,2},{6,4},{8,6},{10,8},{12,10},{14,12},{16,14},{18,16},{20... | collective-permute-start | bytes 589832 | tf_op jit(solution)/shard_map/while/body/eval_jaxpr/ppermute | solution.py:18
  96.6 8.1 %collective-permute-start = (f32[64,768]{1,0:T(8,128)}, f32[64,768]{1,0:T(8,128)S(1)}, u32[]{:S(2)}, u32[]{:S(2)}) collective-permute-start(f32[64,768]{1,0:T(8,128)} %get-tuple-element.616), channel_id=1, source_target_pairs={{2,0},{4,2},{6,4},{8,6},{10,8},{12,10},{14,12},{16,14},{18,16},{20... | collective-permute-start | bytes 589832 | tf_op jit(solution)/shard_map/while/body/eval_jaxpr/ppermute | solution.py:18
  105.4 8.1 %collective-permute-start = (f32[64,768]{1,0:T(8,128)}, f32[64,768]{1,0:T(8,128)S(1)}, u32[]{:S(2)}, u32[]{:S(2)}) collective-permute-start(f32[64,768]{1,0:T(8,128)} %get-tuple-element.616), channel_id=1, source_target_pairs={{2,0},{4,2},{6,4},{8,6},{10,8},{12,10},{14,12},{16,14},{18,16},{20... | collective-permute-start | bytes 589832 | tf_op jit(solution)/shard_map/while/body/eval_jaxpr/ppermute | solution.py:18
  114.2 8.1 %collective-permute-start = (f32[64,768]{1,0:T(8,128)}, f32[64,768]{1,0:T(8,128)S(1)}, u32[]{:S(2)}, u32[]{:S(2)}) collective-permute-start(f32[64,768]{1,0:T(8,128)} %get-tuple-element.616), channel_id=1, source_target_pairs={{2,0},{4,2},{6,4},{8,6},{10,8},{12,10},{14,12},{16,14},{18,16},{20... | collective-permute-start | bytes 589832 | tf_op jit(solution)/shard_map/while/body/eval_jaxpr/ppermute | solution.py:18
  122.9 8.1 %collective-permute-start = (f32[64,768]{1,0:T(8,128)}, f32[64,768]{1,0:T(8,128)S(1)}, u32[]{:S(2)}, u32[]{:S(2)}) collective-permute-start(f32[64,768]{1,0:T(8,128)} %get-tuple-element.616), channel_id=1, source_target_pairs={{2,0},{4,2},{6,4},{8,6},{10,8},{12,10},{14,12},{16,14},{18,16},{20... | collective-permute-start | bytes 589832 | tf_op jit(solution)/shard_map/while/body/eval_jaxpr/ppermute | solution.py:18
  131.7 8.1 %collective-permute-start = (f32[64,768]{1,0:T(8,128)}, f32[64,768]{1,0:T(8,128)S(1)}, u32[]{:S(2)}, u32[]{:S(2)}) collective-permute-start(f32[64,768]{1,0:T(8,128)} %get-tuple-element.616), channel_id=1, source_target_pairs={{2,0},{4,2},{6,4},{8,6},{10,8},{12,10},{14,12},{16,14},{18,16},{20... | collective-permute-start | bytes 589832 | tf_op jit(solution)/shard_map/while/body/eval_jaxpr/ppermute | solution.py:18
  140.5 111.8 %collective-permute-start = (f32[64,768]{1,0:T(8,128)}, f32[64,768]{1,0:T(8,128)S(1)}, u32[]{:S(2)}, u32[]{:S(2)}) collective-permute-start(f32[64,768]{1,0:T(8,128)} %get-tuple-element.616), channel_id=1, source_target_pairs={{2,0},{4,2},{6,4},{8,6},{10,8},{12,10},{14,12},{16,14},{18,16},{20... | collective-permute-start | bytes 589832 | tf_op jit(solution)/shard_map/while/body/eval_jaxpr/ppermute | solution.py:18
  252.3 4.3 copy-start.2
  252.3 0.7 copy-start.10
  256.5 1.6 copy-start.5
  258.1 0.7 copy-start.6
  259.9 0.9 copy-start.3
  260.5 1.8 copy-start.7
  261.6 0.7 copy-start.9
  262.3 3.5 collective-permute-start
  268.7 0.7 copy-start.23
  268.7 0.7 copy-start.27
  268.7 1.4 copy-start.20
  268.8 4.1 copy-start.16
  268.8 69.3 %reduce-scatter.17.cloned.1.call-start = ((), (), s32[]{:S(2)}) async-start(), calls=%async_computation.12 | async-start | bytes 3538944 | tf_op jit(solution)/shard_map/reduce_scatter | solution.py:258
  274.8 0.9 copy-start.12
  274.8 100.3 %reduce-scatter.13.cloned.1.call-start = ((), (), s32[]{:S(2)}) async-start(), calls=%async_computation.10 | async-start | bytes 3538944 | tf_op jit(solution)/shard_map/reduce_scatter | solution.py:257
  277.8 0.9 copy-start.13
  277.8 0.9 copy-start.19
  277.8 0.9 copy-start.25
  277.9 134.2 %reduce-scatter.9.cloned.1.call-start = ((), (), s32[]{:S(2)}) async-start(), calls=%async_computation.8 | async-start | bytes 3538944 | tf_op jit(solution)/shard_map/reduce_scatter | solution.py:256
  280.8 193.0 %reduce-scatter.23.cloned.1.call-start = ((), (), s32[]{:S(2)}) async-start(), calls=%async_computation.15 | async-start | bytes 1253376 | tf_op jit(solution)/shard_map/reduce_scatter | solution.py:265
  301.0 233.5 %reduce-scatter.19.cloned.1.call-start = ((), (), s32[]{:S(2)}) async-start(), calls=%async_computation.13 | async-start | bytes 1253376 | tf_op jit(solution)/shard_map/reduce_scatter | solution.py:264
  338.1 257.2 %reduce-scatter.15.cloned.1.call-start = ((), (), s32[]{:S(2)}) async-start(), calls=%async_computation.11 | async-start | bytes 1253376 | tf_op jit(solution)/shard_map/reduce_scatter | solution.py:263
  375.1 281.0 %reduce-scatter.11.cloned.1.call-start = ((), (), s32[]{:S(2)}) async-start(), calls=%async_computation.9 | async-start | bytes 1253376 | tf_op jit(solution)/shard_map/reduce_scatter | solution.py:262
Sparse Core Ops, SparseCore 0:
  268.9 32.0 reduce-scatter.20
  303.2 34.7 reduce-scatter.16
  340.3 34.7 reduce-scatter.12
  377.2 34.7 reduce-scatter.8
  415.5 58.2 reduce-scatter.22
  477.3 57.1 reduce-scatter.18
  538.1 57.1 reduce-scatter.14
  598.9 57.1 reduce-scatter.10
where the time goes:
time: 666 us; the launch traced here: 665 us
  waiting for transfers between devices  529 us (79%)
  blocking collectives  39.5 us (6%)
  local copies, waits for them, and re-layouts  23.3 us (3%)
  matrix products  22.1 us (3%)
  starting transfers between devices  20.8 us (3%)
  between operations  15.8 us (2%)
  other arithmetic  14.1 us (2%)
    ppermute x16, waiting for transfers between devices, from_behind(): lax.ppermute(value, axis, [(source, source + steps) for source in range(i...  198 us
    reduce_scatter x1, waiting for transfers between devices, on_device(): lax.psum_scatter(column_part[0], 'tm', scatter_dimension=0, tiled=True)  59.3 us
    reduce_scatter x1, waiting for transfers between devices, on_device(): lax.psum_scatter(column_part[1], 'tm', scatter_dimension=0, tiled=True)  59.3 us
    reduce_scatter x1, waiting for transfers between devices, on_device(): lax.psum_scatter(column_part[2], 'tm', scatter_dimension=0, tiled=True)  59.2 us
    psum x1, blocking collectives, on_device(): gain_sum = lax.psum(sum_gain, ('tm', 'video'))  39.5 us
    reduce_scatter x1, waiting for transfers between devices, on_device(): lax.psum_scatter(sum_value, 'video', scatter_dimension=1, tiled=True)  37 us
    reduce_scatter x1, waiting for transfers between devices, on_device(): lax.psum_scatter(sum_key, 'video', scatter_dimension=1, tiled=True)  37 us
    reduce_scatter x1, waiting for transfers between devices, on_device(): lax.psum_scatter(sum_query, 'video', scatter_dimension=1, tiled=True)  36.9 us
  transfers between devices with their start and end apart: 24, of which 24 were waited for; matrix products, arithmetic and copies ran while one was open for 2% of the time, Pallas kernels for 0%

commit v1 on v0

v1 whole, which is shorter than its diff:
```python
import functools
import math

import jax
import jax.numpy as jnp
from jax import lax
from jax.experimental import pallas as pl
from jax.experimental.pallas import tpu as pltpu
from jax.sharding import PartitionSpec as P

NORM_EPSILON = 1e-06
MESH = pl.DeviceIdType.MESH
F32 = jnp.float32
BF16 = jnp.bfloat16
NN = (((1,), (0,)), ((), ()))
NT = (((1,), (1,)), ((), ()))
TN = (((0,), (0,)), ((), ()))
CHUNKS = 2


def dot(left, right, form):
    return lax.dot_general(left, right, form, preferred_element_type=F32)


def key_rows(frame_rows, offset, position):
    length, features = frame_rows.shape
    within = jnp.arange(length, dtype=jnp.int32)
    frame_time = (offset + position * length + within).astype(F32)
    half_width = features // 2
    frequency = 0.0625 * jnp.exp(-math.log(1000.0) * jnp.arange(half_width, dtype=F32) / half_width)
    phases = frame_time[:, None] * frequency
    return frame_rows + jnp.concatenate([jnp.sin(phases), jnp.cos(phases)], axis=-1)


def group_member(groups, g):
    me = lax.axis_index("tm")
    return {"video": lax.div(g, 2), "tm": (me // 2) * 2 + lax.rem(g, 2)}


def chain_kernel(
    owners, groups, heads,
    slot_ref, mem_ref, keyin_ref, cot_ref, bias_ref, gain_ref, wq_ref, wk_ref, wv_ref, wo_ref,
    grad_ref, a1_ref, a2_ref, b1_ref, b2_ref, gsum_ref,
    incoming, mine, prob, half, kbd, vbd, qp, att_all, sg_all, og_all, qg_all, unit_ref, inv_ref,
    chain_send, chain_recv, a_send, a_recv,
):
    me = lax.axis_index("tm")
    vid = lax.axis_index("video")
    rows, features = mem_ref.shape
    length = keyin_ref.shape[0]
    head = features // heads
    pairs = heads // 2
    pw = 2 * head
    members = 2 * groups
    g_me = vid * 2 + lax.rem(me, 2)
    scale = head ** (-0.5)

    barrier = pltpu.get_barrier_semaphore()
    for off in range(1, members):
        pl.semaphore_signal(barrier, inc=1, device_id=group_member(groups, lax.rem(g_me + off, members)), device_id_type=MESH)

    @pl.when(me > 0)
    def _():
        pl.semaphore_signal(barrier, inc=1, device_id={"tm": me - 1}, device_id_type=MESH)

    @pl.when(me < owners - 1)
    def _():
        pl.semaphore_signal(barrier, inc=1, device_id={"tm": me + 1}, device_id_type=MESH)

    ends = jnp.where(me > 0, 1, 0) + jnp.where(me < owners - 1, 1, 0)
    pl.semaphore_wait(barrier, members - 1 + ends)

    def a_copy(which, src, dst, off):
        g = lax.rem(g_me + off, members)
        return pltpu.make_async_remote_copy(
            src_ref=src, dst_ref=dst.at[g_me], send_sem=a_send.at[which, off], recv_sem=a_recv.at[which, g_me],
            device_id=group_member(groups, g), device_id_type=MESH,
        )

    for off in range(1, members):
        a_copy(0, keyin_ref, a1_ref, off).start()
    a1_ref[g_me] = keyin_ref[...]

    mem = mem_ref[...].astype(F32)
    inv = lax.rsqrt(jnp.mean(mem * mem, axis=-1, keepdims=True) + NORM_EPSILON)
    unit = mem * inv
    unit_ref[...] = unit
    inv_ref[...] = jnp.broadcast_to(inv, inv_ref.shape)
    normed = (unit * gain_ref[...]).astype(BF16)
    mine[1] = normed.astype(F32)
    keyin = keyin_ref[...].astype(BF16)
    qp[...] = dot(normed, wq_ref[...], NN).astype(BF16)
    kp = dot(keyin, wk_ref[...], NN).astype(BF16)
    vp = dot(keyin, wv_ref[...], NN).astype(BF16)
    low = lax.broadcasted_iota(jnp.int32, (length, pw), 1) < head
    zero = jnp.zeros((length, pw), BF16)
    for p in range(pairs):
        kk = kp[:, p * pw:(p + 1) * pw]
        vv = vp[:, p * pw:(p + 1) * pw]
        kbd[p, :length] = jnp.where(low, kk, zero)
        kbd[p, length:] = jnp.where(low, zero, kk)
        vbd[p, :length] = jnp.where(low, vv, zero)
        vbd[p, length:] = jnp.where(low, zero, vv)
    for p in range(pairs):
        s2 = dot(qp[:, p * pw:(p + 1) * pw], kbd[p], NT)
        for q in range(2):
            h = 2 * p + q
            s = s2[:, q * length:(q + 1) * length] * scale + bias_ref[h:h + 1, :]
            e = jnp.exp(s - jnp.max(s, axis=-1, keepdims=True))
            pr = e / jnp.sum(e, axis=-1, keepdims=True)
            prob[:, h * length:(h + 1) * length] = pr
            half[:, h * length:(h + 1) * length] = pr.astype(BF16)
        mine[0, :, p * pw:(p + 1) * pw] = dot(half[:, p * 2 * length:(p + 1) * 2 * length], vbd[p], NN).astype(BF16).astype(F32)

    for off in range(1, members):
        g = lax.rem(g_me + off, members)
        a_copy(1, mine.at[lax.rem(g, 2)], a2_ref, off).start()
    a2_ref[g_me] = mine[lax.rem(me, 2)]

    live = slot_ref[0].astype(F32)
    step = rows // CHUNKS

    def chain_copy(c):
        return pltpu.make_async_remote_copy(
            src_ref=grad_ref.at[pl.ds(c * step, step)], dst_ref=incoming.at[pl.ds(c * step, step)],
            send_sem=chain_send.at[c], recv_sem=chain_recv.at[c],
            device_id={"tm": jnp.maximum(me - 1, 0)}, device_id_type=MESH,
        )

    @pl.when(me == owners - 1)
    def _():
        incoming[...] = jnp.zeros_like(incoming)

    gain_total = jnp.zeros((1, features), F32)
    for c in range(CHUNKS):
        r = slice(c * step, (c + 1) * step)

        @pl.when(me < owners - 1)
        def _():
            chain_copy(c).wait_recv()

        grad_in = incoming[r, :] + cot_ref[r, :].astype(F32)
        og = (live * grad_in).astype(BF16)
        og_all[r, :] = og
        att = dot(og, wo_ref[...], NT).astype(BF16)
        att_all[r, :] = att
        for p in range(pairs):
            pg2 = dot(att[:, p * pw:(p + 1) * pw], vbd[p], NT)
            for q in range(2):
                h = 2 * p + q
                pg = pg2[:, q * length:(q + 1) * length]
                pr = prob[r, h * length:(h + 1) * length]
                inner = jnp.sum(pr * pg, axis=-1, keepdims=True)
                sg_all[r, h * length:(h + 1) * length] = (pr * (pg - inner) * scale).astype(BF16)
            qg_all[r, p * pw:(p + 1) * pw] = dot(sg_all[r, p * 2 * length:(p + 1) * 2 * length], kbd[p], NN).astype(BF16)
        ng = dot(qg_all[r, :], wq_ref[...], NT)
        un = unit_ref[r, :]
        gain_total = gain_total + jnp.sum(ng * un, axis=0, keepdims=True)
        sc = ng * gain_ref[...]
        grad_ref[r, :] = grad_in + inv_ref[r, 0:1] * (sc - un * jnp.mean(sc * un, axis=-1, keepdims=True))

        @pl.when(me > 0)
        def _():
            chain_copy(c).start()

    gsum_ref[...] = gain_total

    width = features // groups
    lowr = lax.broadcasted_iota(jnp.int32, (rows, pw), 1) < head
    zr = jnp.zeros((rows, pw), BF16)

    def put(out, which, p, value):
        for v in range(groups):
            lo, hi = max(p * pw, v * width), min((p + 1) * pw, (v + 1) * width)
            if lo < hi:
                out[which, v, :, lo - v * width:hi - v * width] = value[:, lo - p * pw:hi - p * pw]

    for p in range(pairs):
        for which, (left_ref, right_ref) in enumerate(((sg_all, qp), (half, att_all))):
            right = right_ref[:, p * pw:(p + 1) * pw]
            right = jnp.concatenate([jnp.where(lowr, right, zr), jnp.where(lowr, zr, right)], axis=0)
            base = 2 * p * length
            left = jnp.concatenate([left_ref[:, base:base + length], left_ref[:, base + length:base + 2 * length]], axis=0)
            put(b1_ref, which, p, dot(left, right, TN).astype(BF16).astype(F32))
        put(b2_ref, 0, p, og_all[:, p * pw:(p + 1) * pw].astype(F32))
        put(b2_ref, 1, p, qg_all[:, p * pw:(p + 1) * pw].astype(F32))

    @pl.when(me > 0)
    def _():
        for c in range(CHUNKS):
            chain_copy(c).wait_send()

    for off in range(1, members):
        g = lax.rem(g_me + members - off, members)
        for which, dst in ((0, a1_ref), (1, a2_ref)):
            a_copy(which, dst.at[g_me], dst, off).wait_send()
            pltpu.make_async_remote_copy(
                src_ref=dst.at[g], dst_ref=dst.at[g], send_sem=a_send.at[which, off], recv_sem=a_recv.at[which, g],
                device_id=group_member(groups, g), device_id_type=MESH,
            ).wait_recv()


def reduce_kernel(
    owners, groups,
    a1_ref, a2_ref, b1_ref, b2_ref, gsum_ref,
    out_ref, gain_ref,
    s1, s2, t1, t2, acc, final, gslot, gquad, *rest,
):
    me = lax.axis_index("tm")
    vid = lax.axis_index("video")
    members = 2 * groups
    chips = owners // 2
    bits = chips.bit_length() - 1
    lands = rest[:bits]
    b_send, b_recv, r_send, r_recv, q_send, q_recv, f_send, f_recv = rest[bits:]
    chip, core = me // 2, lax.rem(me, 2)
    g_me = vid * 2 + core
    pieces, features, pw = acc.shape
    per = pieces // 2
    block = features // chips
    part = block // 2
    scale = 1.0 / (owners * groups)

    barrier = pltpu.get_barrier_semaphore()
    for off in range(1, members):
        pl.semaphore_signal(barrier, inc=1, device_id=group_member(groups, lax.rem(g_me + off, members)), device_id_type=MESH)
    for off in range(1, chips):
        pl.semaphore_signal(barrier, inc=1, device_id={"tm": lax.rem(me + 2 * off, owners)}, device_id_type=MESH)
    pl.semaphore_wait(barrier, members - 1 + chips - 1)

    def b_copy(which, off):
        g = lax.rem(g_me + off, members)
        v, c = lax.div(g, 2), lax.rem(g, 2)
        src, dst = ((b1_ref.at[c, v], s1), (b2_ref.at[c, v], s2), (gsum_ref, gslot))[which]
        return pltpu.make_async_remote_copy(
            src_ref=src, dst_ref=dst.at[g_me], send_sem=b_send.at[which, off], recv_sem=b_recv.at[which, g_me],
            device_id=group_member(groups, g), device_id_type=MESH,
        )

    def b_arrive(which, off):
        g = lax.rem(g_me + members - off, members)
        dst = (s1, s2, gslot)[which]
        return pltpu.make_async_remote_copy(
            src_ref=dst.at[g], dst_ref=dst.at[g], send_sem=b_send.at[which, off], recv_sem=b_recv.at[which, g],
            device_id=group_member(groups, g), device_id_type=MESH,
        )

    for which in (2, 1, 0):
        for off in range(1, members):
            b_copy(which, off).start()
    s1[g_me] = b1_ref[core, vid]
    s2[g_me] = b2_ref[core, vid]
    gslot[g_me] = gsum_ref[...]
    for g in range(members):
        t1[g] = a1_ref[g].astype(BF16)
        t2[g] = a2_ref[g].astype(BF16)

    order = [int(format(i, "b").zfill(bits)[::-1], 2) if bits else 0 for i in range(chips)]

    def products(which):
        slots, left = ((s2, t2), (s1, t1))[which]
        for off in range(1, members):
            b_arrive(1 - which, off).wait_recv()
        flat = left[...].reshape(members * left.shape[1], features)
        for i in range(per):
            right = slots[:, :, i * pw:(i + 1) * pw].reshape(flat.shape[0], pw).astype(BF16)
            value = dot(flat, right, TN)
            for pos in range(chips):
                k = order[pos]
                acc[which * per + i, pos * block:(pos + 1) * block, :] = value[k * block:(k + 1) * block, :]

    starts = []
    lo = 0
    for s in range(bits):
        span = features >> (s + 1)
        bit = lax.rem(lax.div(chip, 2 ** s), 2)
        starts.append((lo + (1 - bit) * span, lo + bit * span, span, chip + (1 - 2 * bit) * 2 ** s))
        lo = lo + bit * span
    home = pl.multiple_of(lo, 8)

    def r_copy(p, s):
        give, _, span, peer = starts[s]
        return pltpu.make_async_remote_copy(
            src_ref=acc.at[p, pl.ds(pl.multiple_of(give, 8), span)], dst_ref=lands[s].at[p],
            send_sem=r_send.at[p, s], recv_sem=r_recv.at[p, s],
            device_id={"tm": peer * 2 + core}, device_id_type=MESH,
        )

    def r_finish(p, s):
        _, keep, span, _ = starts[s]
        r_copy(p, s).wait_recv()
        at = pl.ds(pl.multiple_of(keep, 8), span)
        acc[p, at, :] = acc[p, at, :] + lands[s][p]

    def f_copy(p):
        theirs = pl.ds(pl.multiple_of(lo + (1 - core) * part, 8), part)
        return pltpu.make_async_remote_copy(
            src_ref=acc.at[p, theirs], dst_ref=final.at[p], send_sem=f_send.at[p], recv_sem=f_recv.at[p],
            device_id={"tm": chip * 2 + 1 - core}, device_id_type=MESH,
        )

    for wave in range(pieces + bits):
        if wave == 0:
            products(0)
        if wave == per:
            products(1)
        for s in reversed(range(bits + 1)):
            p = wave - s
            if 0 <= p < pieces:
                if s > 0:
                    r_finish(p, s - 1)
                if s < bits:
                    r_copy(p, s).start()
                else:
                    f_copy(p).start()
        if wave == 0:
            for off in range(1, members):
                b_arrive(2, off).wait_recv()
            gquad[chip] = jnp.sum(gslot[...], axis=0)
            for off in range(1, chips):
                g_copy = pltpu.make_async_remote_copy(
                    src_ref=gquad.at[chip], dst_ref=gquad.at[chip], send_sem=q_send.at[off], recv_sem=q_recv.at[chip],
                    device_id={"tm": lax.rem(me + 2 * off, owners)}, device_id_type=MESH,
                )
                g_copy.start()

    mine_rows = pl.ds(pl.multiple_of(lo + core * part, 8), part)
    for p in range(pieces):
        which, i = p // per, p % per
        cols = slice(i * pw, (i + 1) * pw)
        out_ref[2 * which + core, :, cols] = acc[p, mine_rows, :] * scale
    for p in range(pieces):
        which, i = p // per, p % per
        cols = slice(i * pw, (i + 1) * pw)
        f_copy(p).wait_recv()
        out_ref[2 * which + 1 - core, :, cols] = final[p] * scale

    for off in range(1, chips):
        src = lax.rem(chip + chips - off, chips)
        got = pltpu.make_async_remote_copy(
            src_ref=gquad.at[src], dst_ref=gquad.at[src], send_sem=q_send.at[off], recv_sem=q_recv.at[src],
            device_id={"tm": lax.rem(me + 2 * off, owners)}, device_id_type=MESH,
        )
        got.wait()
    gain_ref[...] = jnp.sum(gquad[...], axis=0) * scale
    for which in range(3):
        for off in range(1, members):
            b_copy(which, off).wait_send()
    for p in range(pieces):
        for s in range(bits):
            r_copy(p, s).wait_send()
        f_copy(p).wait_send()


def on_device(
    memory, frames, mem_cot, slot_used, key_bias, start_offset, norm_gain, w_query, w_key, w_value, w_out
):
    owners = lax.axis_size("tm")
    groups = lax.axis_size("video")
    position = lax.axis_index("tm")
    streams, rows, features = memory.shape[2:]
    length = frames.shape[3]
    heads = key_bias.shape[3]
    members = 2 * groups
    chips = owners // 2
    bits = chips.bit_length() - 1
    width = features // groups
    keyin = key_rows(frames[0, 0, 0], start_offset[0, 0], position)
    vmem = pl.BlockSpec(memory_space=pltpu.VMEM)
    smem = pl.BlockSpec(memory_space=pltpu.SMEM)
    sds = jax.ShapeDtypeStruct
    grad, a1, a2, b1, b2, gsum = pl.pallas_call(
        functools.partial(chain_kernel, owners, groups, heads),
        out_shape=(
            sds((rows, features), F32),
            sds((members, length, features), F32),
            sds((members, rows, features), F32),
            sds((2, groups, length, width), F32),
            sds((2, groups, rows, width), F32),
            sds((1, features), F32),
        ),
        in_specs=[smem] + [vmem] * 9,
        out_specs=(vmem,) * 6,
        scratch_shapes=[
            pltpu.VMEM((rows, features), F32),
            pltpu.VMEM((2, rows, features), F32),
            pltpu.VMEM((rows, heads * length), F32),
            pltpu.VMEM((rows, heads * length), BF16),
            pltpu.VMEM((heads // 2, 2 * length, 2 * features // heads), BF16),
            pltpu.VMEM((heads // 2, 2 * length, 2 * features // heads), BF16),
            pltpu.VMEM((rows, features), BF16),
            pltpu.VMEM((rows, features), BF16),
            pltpu.VMEM((rows, heads * length), BF16),
            pltpu.VMEM((rows, features), BF16),
            pltpu.VMEM((rows, features), BF16),
            pltpu.VMEM((rows, features), F32),
            pltpu.VMEM((rows, 128), F32),
            pltpu.SemaphoreType.DMA((CHUNKS,)),
            pltpu.SemaphoreType.DMA((CHUNKS,)),
            pltpu.SemaphoreType.DMA((2, members)),
            pltpu.SemaphoreType.DMA((2, members)),
        ],
        compiler_params=pltpu.CompilerParams(collective_id=0, has_side_effects=True, vmem_limit_bytes=56 * 1024 * 1024),
        name="chain",
    )(
        slot_used[0, 0], memory[0, 0, 0], keyin, mem_cot[0, 0, 0], key_bias[0, 0, 0],
        norm_gain[None, :], w_query, w_key, w_value, w_out,
    )
    pw = 128 if width % 128 == 0 else width
    pieces = 2 * (width // pw)
    dma = pltpu.SemaphoreType.DMA
    weights, gain = pl.pallas_call(
        functools.partial(reduce_kernel, owners, groups),
        out_shape=(sds((4, features // owners, width), F32), sds((1, features), F32)),
        in_specs=[vmem] * 5,
        out_specs=(vmem,) * 2,
        scratch_shapes=[
            pltpu.VMEM((members, length, width), F32),
            pltpu.VMEM((members, rows, width), F32),
            pltpu.VMEM((members, length, features), BF16),
            pltpu.VMEM((members, rows, features), BF16),
            pltpu.VMEM((pieces, features, pw), F32),
            pltpu.VMEM((pieces, features // owners, pw), F32),
            pltpu.VMEM((members, 1, features), F32),
            pltpu.VMEM((chips, 1, features), F32),
        ]
        + [pltpu.VMEM((pieces, features >> (s + 1), pw), F32) for s in range(bits)]
        + [
            dma((3, members)), dma((3, members)), dma((pieces, bits)), dma((pieces, bits)),
            dma((chips,)), dma((chips,)), dma((pieces,)), dma((pieces,)),
        ],
        compiler_params=pltpu.CompilerParams(collective_id=1, has_side_effects=True, vmem_limit_bytes=56 * 1024 * 1024),
        name="reduce",
    )(a1, a2, b1, b2, gsum)
    return (grad[None, None, None], weights[1], weights[2], weights[3], weights[0], gain[0])


def solution(mesh):
    return jax.shard_map(
        on_device,
        mesh=mesh,
        in_specs=(
            P("video", "tm", None, None, None),
            P("video", "tm", None, None, None),
            P("video", "tm", None, None, None),
            P("video", "tm", None),
            P("video", "tm", None, None, None),
            P("video", None),
            P(),
            P(),
            P(),
            P(),
            P(),
        ),
        out_specs=(
            P("video", "tm", None, None, None),
            P("tm", "video"),
            P("tm", "video"),
            P("tm", "video"),
            P("tm", "video"),
            P(),
        ),
        check_vma=False,
    )
```

time: 666 us -> 150 us (0.23)
  waiting for transfers between devices: 529 us -> 0 us
  Pallas kernels: 0 us -> 139 us
  blocking collectives: 39.5 us -> 0 us
  matrix products: 22.1 us -> 0 us
  starting transfers between devices: 20.8 us -> 0 us
  local copies, waits for them, and re-layouts: 23.3 us -> 4.95 us
  between operations: 15.8 us -> 1.97 us
  other arithmetic: 14.1 us -> 3.85 us
    reduce_scatter x8 -> x0, waiting for transfers between devices: 330 us -> none  [the longest x1 59.3 us: on_device(): lax.psum_scatter(column_part[0], 'tm', scatter_dimension=0, tiled=True)]
    ppermute x16 -> x0, waiting for transfers between devices: 198 us -> none  [from_behind(): lax.ppermute(value, axis, [(source, source + steps) for source in range(i...]
    pallas_call x0 -> x2, Pallas kernels: none -> 139 us  [the longest x1 84.4 us: on_device(): pl.pallas_call(functools.partial(chain_kernel, owners, groups, heads), ou...]
    psum x1 -> x0, blocking collectives: 39.5 us -> none  [on_device(): gain_sum = lax.psum(sum_gain, ('tm', 'video'))]
    dot_general x15 -> x0, matrix products: 22.1 us -> none  [product(): return jnp.einsum(form, left, right, preferred_element_type=jnp.float32)]
    ppermute x16 -> x0, starting transfers between devices: 20.5 us -> none  [from_behind(): lax.ppermute(value, axis, [(source, source + steps) for source in range(i...]
    another operation x19 -> x0, local copies, waits for them, and re-layouts: 11.4 us -> none
    mul x7 -> x1, other arithmetic: 7.67 us -> 0.01 us  [key_rows(): 0.0625 * jnp.exp(-math.log(1000.0) * jnp.arange(half_width, dtype=F32) /...]
  transfers between devices with their start and end apart: 24 -> 0, of which waited for: 24 -> 0; matrix products, arithmetic and copies ran while one was open for 2% -> 0% of each run, Pallas kernels for 0% -> 0%
where the time goes in v1:
time: 150 us
  Pallas kernels  139 us (93%)
  local copies, waits for them, and re-layouts  4.95 us (3%)
  other arithmetic  3.85 us (3%)
  between operations  1.97 us (1%)
    pallas_call x1, Pallas kernels, on_device(): pl.pallas_call(functools.partial(chain_kernel, owners, groups, heads), ou...  84.4 us
    pallas_call x1, Pallas kernels, on_device(): pl.pallas_call(functools.partial(reduce_kernel, owners, groups), out_shap...  54.4 us

profile of v1, /device:TPU:0, one launch (start us, length us, event | category | flops | bytes accessed | tf_op | source)
XLA Modules:
  0.0 149.7 jit_solution(11746743959253785068)
XLA Ops:
  2.0 1.3 broadcast_in_dim.8.gain_ref
  3.2 1.3 copy.19
  4.5 0.8 multiply_sine_fusion
  5.3 1.8 %maximum_add_fusion.keyin_ref = f32[128,768]{1,0:T(8,128)} fusion(f32[128,384]{1,0:T(8,128)S(1)} %get-tuple-element.27, f32[128,384]{1,0:T(8,128)S(1)} %get-tuple-element.26, f32[1,1,1,128,768]{4,3,2,1,0:T(8,128)} %param.12), kind=kLoop, calls=%fused_computation | loop fusion | flops 196608 | bytes 1179648 | tf_op jit(solution)/shard_map/add | solution.py:32
  7.1 84.4 %chain.1 = (f32[64,768]{1,0:T(8,128)}, f32[4,128,768]{2,1,0:T(8,128)}, f32[4,64,768]{2,1,0:T(8,128)}, f32[2,2,128,384]{3,2,1,0:T(8,128)}, f32[2,2,64,384]{3,2,1,0:T(8,128)}, /*index=5*/f32[1,768]{1,0:T(1,128)}) custom-call(s32[1]{0:T(128)} %bitcast.18.slot_ref, bf16[64,768]{1,0:T(8,128)(2,1)} %bitcast.21, f32[128,768]{1,0:T(8,128)} %maximum_add_fusion.keyin_ref, ...), custom_call_target="tpu_custom_call" | custom-call | tf_op jit(solution)/shard_map/chain/pallas_call | solution.py:372
  91.5 0.0 copy-start
  91.5 54.4 %reduce.2 = (f32[4,48,384]{2,1,0:T(8,128)}, f32[1,768]{1,0:T(1,128)}) custom-call(f32[4,128,768]{2,1,0:T(8,128)} %get-tuple-element.15.a1_ref, f32[4,64,768]{2,1,0:T(8,128)} %get-tuple-element.16.a2_ref, f32[2,2,128,384]{3,2,1,0:T(8,128)} %get-tuple-element.17.b1_ref, f32[2,2,64,384]{3,2,1,0:T(8,128)} %get-tuple-element.18.b2_ref, ...), custom_call_target="tpu_custom_call" | custom-call | tf_op jit(solution)/shard_map/reduce/pallas_call | solution.py:412
  146.0 1.7 %slice_bitcast_fusion = (f32[48,384]{1,0:T(8,128)}, f32[48,384]{1,0:T(8,128)}, f32[48,384]{1,0:T(8,128)}, f32[48,384]{1,0:T(8,128)}) fusion(f32[4,48,384]{2,1,0:T(8,128)} %get-tuple-element.20), kind=kLoop, calls=%fused_computation.3 | loop fusion | bytes 589824 | tf_op jit(solution)/shard_map/squeeze | solution.py:435
  147.7 1.3 reduce.1
  149.0 0.0 copy-done
  149.0 0.7 copy.23
  (2 shorter events, 0.0 us)
Async XLA Ops:
  91.5 57.5 %copy-start = (f32[64,768]{1,0:T(8,128)S(1)}, f32[64,768]{1,0:T(8,128)}, u32[]{:S(2)}) copy-start(f32[64,768]{1,0:T(8,128)} %get-tuple-element.14) | copy-start | bytes 589828

commit v2 on v1

--- a/solution.py
+++ b/solution.py
@@ -15,7 +15,7 @@
 NN = (((1,), (0,)), ((), ()))
 NT = (((1,), (1,)), ((), ()))
 TN = (((0,), (0,)), ((), ()))
-CHUNKS = 2
+CHUNKS = 4
 
 
 def dot(left, right, form):
@@ -220,6 +220,7 @@
     block = features // chips
     part = block // 2
     scale = 1.0 / (owners * groups)
+    length, rows = a1_ref.shape[1], a2_ref.shape[1]
 
     barrier = pltpu.get_barrier_semaphore()
     for off in range(1, members):
@@ -252,8 +253,10 @@
     s2[g_me] = b2_ref[core, vid]
     gslot[g_me] = gsum_ref[...]
     for g in range(members):
-        t1[g] = a1_ref[g].astype(BF16)
-        t2[g] = a2_ref[g].astype(BF16)
+        t1[:, g * length:(g + 1) * length] = jnp.transpose(a1_ref[g]).astype(BF16)
+    for g in range(0, members, 2):
+        both = jnp.concatenate([a2_ref[g], a2_ref[g + 1]], axis=0)
+        t2[:, g * rows:(g + 2) * rows] = jnp.transpose(both).astype(BF16)
 
     order = [int(format(i, "b").zfill(bits)[::-1], 2) if bits else 0 for i in range(chips)]
 
@@ -261,10 +264,9 @@
         slots, left = ((s2, t2), (s1, t1))[which]
         for off in range(1, members):
             b_arrive(1 - which, off).wait_recv()
-        flat = left[...].reshape(members * left.shape[1], features)
         for i in range(per):
-            right = slots[:, :, i * pw:(i + 1) * pw].reshape(flat.shape[0], pw).astype(BF16)
-            value = dot(flat, right, TN)
+            right = slots[:, :, i * pw:(i + 1) * pw].reshape(left.shape[1], pw).astype(BF16)
+            value = dot(left[...], right, NN)
             for pos in range(chips):
                 k = order[pos]
                 acc[which * per + i, pos * block:(pos + 1) * block, :] = value[k * block:(k + 1) * block, :]
@@ -417,8 +419,8 @@
         scratch_shapes=[
             pltpu.VMEM((members, length, width), F32),
             pltpu.VMEM((members, rows, width), F32),
-            pltpu.VMEM((members, length, features), BF16),
-            pltpu.VMEM((members, rows, features), BF16),
+            pltpu.VMEM((features, members * length), BF16),
+            pltpu.VMEM((features, members * rows), BF16),
             pltpu.VMEM((pieces, features, pw), F32),
             pltpu.VMEM((pieces, features // owners, pw), F32),
             pltpu.VMEM((members, 1, features), F32),

time: 150 us -> 149 us (level)
  no operation moved by 1% of the time
where the time goes in v2:
time: 149 us
  Pallas kernels  138 us (93%)
  local copies, waits for them, and re-layouts  4.95 us (3%)
  other arithmetic  3.85 us (3%)
  between operations  1.97 us (1%)
    pallas_call x1, Pallas kernels, on_device(): pl.pallas_call(functools.partial(chain_kernel, owners, groups, heads), ou...  83.9 us
    pallas_call x1, Pallas kernels, on_device(): pl.pallas_call(functools.partial(reduce_kernel, owners, groups), out_shap...  54.4 us

profile of v2, /device:TPU:0, one launch (start us, length us, event | category | flops | bytes accessed | tf_op | source)
XLA Modules:
  0.0 149.1 jit_solution(6552939817461147159)
XLA Ops:
  2.0 1.3 broadcast_in_dim.8.gain_ref
  3.2 1.3 copy.19
  4.5 0.8 multiply_sine_fusion
  5.3 1.8 %maximum_add_fusion.keyin_ref = f32[128,768]{1,0:T(8,128)} fusion(f32[128,384]{1,0:T(8,128)S(1)} %get-tuple-element.27, f32[128,384]{1,0:T(8,128)S(1)} %get-tuple-element.26, f32[1,1,1,128,768]{4,3,2,1,0:T(8,128)} %param.12), kind=kLoop, calls=%fused_computation | loop fusion | flops 196608 | bytes 1179648 | tf_op jit(solution)/shard_map/add | solution.py:32
  7.1 83.9 %chain.1 = (f32[64,768]{1,0:T(8,128)}, f32[4,128,768]{2,1,0:T(8,128)}, f32[4,64,768]{2,1,0:T(8,128)}, f32[2,2,128,384]{3,2,1,0:T(8,128)}, f32[2,2,64,384]{3,2,1,0:T(8,128)}, /*index=5*/f32[1,768]{1,0:T(1,128)}) custom-call(s32[1]{0:T(128)} %bitcast.18.slot_ref, bf16[64,768]{1,0:T(8,128)(2,1)} %bitcast.21, f32[128,768]{1,0:T(8,128)} %maximum_add_fusion.keyin_ref, ...), custom_call_target="tpu_custom_call" | custom-call | tf_op jit(solution)/shard_map/chain/pallas_call | solution.py:374
  91.0 0.0 copy-start
  91.0 54.4 %reduce.2 = (f32[4,48,384]{2,1,0:T(8,128)}, f32[1,768]{1,0:T(1,128)}) custom-call(f32[4,128,768]{2,1,0:T(8,128)} %get-tuple-element.15.a1_ref, f32[4,64,768]{2,1,0:T(8,128)} %get-tuple-element.16.a2_ref, f32[2,2,128,384]{3,2,1,0:T(8,128)} %get-tuple-element.17.b1_ref, f32[2,2,64,384]{3,2,1,0:T(8,128)} %get-tuple-element.18.b2_ref, ...), custom_call_target="tpu_custom_call" | custom-call | tf_op jit(solution)/shard_map/reduce/pallas_call | solution.py:414
  145.4 1.7 %slice_bitcast_fusion = (f32[48,384]{1,0:T(8,128)}, f32[48,384]{1,0:T(8,128)}, f32[48,384]{1,0:T(8,128)}, f32[48,384]{1,0:T(8,128)}) fusion(f32[4,48,384]{2,1,0:T(8,128)} %get-tuple-element.20), kind=kLoop, calls=%fused_computation.3 | loop fusion | bytes 589824 | tf_op jit(solution)/shard_map/squeeze | solution.py:437
  147.1 1.3 reduce.1
  148.4 0.0 copy-done
  148.4 0.7 copy.23
  (2 shorter events, 0.0 us)
Async XLA Ops:
  91.0 57.4 %copy-start = (f32[64,768]{1,0:T(8,128)S(1)}, f32[64,768]{1,0:T(8,128)}, u32[]{:S(2)}) copy-start(f32[64,768]{1,0:T(8,128)} %get-tuple-element.14) | copy-start | bytes 589828

commit v3 on v2

--- a/solution.py
+++ b/solution.py
@@ -37,15 +37,21 @@
     return {"video": lax.div(g, 2), "tm": (me // 2) * 2 + lax.rem(g, 2)}
 
 
-def chain_kernel(
+def whole_kernel(
     owners, groups, heads,
     slot_ref, mem_ref, keyin_ref, cot_ref, bias_ref, gain_ref, wq_ref, wk_ref, wv_ref, wo_ref,
-    grad_ref, a1_ref, a2_ref, b1_ref, b2_ref, gsum_ref,
-    incoming, mine, prob, half, kbd, vbd, qp, att_all, sg_all, og_all, qg_all, unit_ref, inv_ref,
+    grad_ref, out_ref, gain_out_ref,
+    a1_ref, a2_ref, b1_ref, b2_ref, gsum_ref,
+    incoming, mine, prob, half, kbd, vbd, qp, att_all, sg_all, og_all, qg_all, unit_ref, inv_ref, wot, wqt,
     chain_send, chain_recv, a_send, a_recv,
+    *reduce_scratch,
 ):
     me = lax.axis_index("tm")
     vid = lax.axis_index("video")
+    chips = owners // 2
+    bits = chips.bit_length() - 1
+    chip, core = me // 2, lax.rem(me, 2)
+    peers = [chip + (1 - 2 * lax.rem(lax.div(chip, 2 ** b), 2)) * 2 ** b for b in range(bits)]
     rows, features = mem_ref.shape
     length = keyin_ref.shape[0]
     head = features // heads
@@ -59,6 +65,9 @@
     for off in range(1, members):
         pl.semaphore_signal(barrier, inc=1, device_id=group_member(groups, lax.rem(g_me + off, members)), device_id_type=MESH)
 
+    for peer in peers:
+        pl.semaphore_signal(barrier, inc=1, device_id={"tm": peer * 2 + core}, device_id_type=MESH)
+
     @pl.when(me > 0)
     def _():
         pl.semaphore_signal(barrier, inc=1, device_id={"tm": me - 1}, device_id_type=MESH)
@@ -68,7 +77,7 @@
         pl.semaphore_signal(barrier, inc=1, device_id={"tm": me + 1}, device_id_type=MESH)
 
     ends = jnp.where(me > 0, 1, 0) + jnp.where(me < owners - 1, 1, 0)
-    pl.semaphore_wait(barrier, members - 1 + ends)
+    pl.semaphore_wait(barrier, members - 1 + bits + ends)
 
     def a_copy(which, src, dst, off):
         g = lax.rem(g_me + off, members)
@@ -101,6 +110,8 @@
         kbd[p, length:] = jnp.where(low, zero, kk)
         vbd[p, :length] = jnp.where(low, vv, zero)
         vbd[p, length:] = jnp.where(low, zero, vv)
+    wot[...] = jnp.transpose(wo_ref[...])
+    wqt[...] = jnp.transpose(wq_ref[...])
     for p in range(pairs):
         s2 = dot(qp[:, p * pw:(p + 1) * pw], kbd[p], NT)
         for q in range(2):
@@ -142,7 +153,7 @@
         grad_in = incoming[r, :] + cot_ref[r, :].astype(F32)
         og = (live * grad_in).astype(BF16)
         og_all[r, :] = og
-        att = dot(og, wo_ref[...], NT).astype(BF16)
+        att = dot(og, wot[...], NN).astype(BF16)
         att_all[r, :] = att
         for p in range(pairs):
             pg2 = dot(att[:, p * pw:(p + 1) * pw], vbd[p], NT)
@@ -153,7 +164,7 @@
                 inner = jnp.sum(pr * pg, axis=-1, keepdims=True)
                 sg_all[r, h * length:(h + 1) * length] = (pr * (pg - inner) * scale).astype(BF16)
             qg_all[r, p * pw:(p + 1) * pw] = dot(sg_all[r, p * 2 * length:(p + 1) * 2 * length], kbd[p], NN).astype(BF16)
-        ng = dot(qg_all[r, :], wq_ref[...], NT)
+        ng = dot(qg_all[r, :], wqt[...], NN)
         un = unit_ref[r, :]
         gain_total = gain_total + jnp.sum(ng * un, axis=0, keepdims=True)
         sc = ng * gain_ref[...]
@@ -185,26 +196,31 @@
         put(b2_ref, 0, p, og_all[:, p * pw:(p + 1) * pw].astype(F32))
         put(b2_ref, 1, p, qg_all[:, p * pw:(p + 1) * pw].astype(F32))
 
+    def a_arrive():
+        for off in range(1, members):
+            g = lax.rem(g_me + members - off, members)
+            for which, dst in ((0, a1_ref), (1, a2_ref)):
+                a_copy(which, dst.at[g_me], dst, off).wait_send()
+                pltpu.make_async_remote_copy(
+                    src_ref=dst.at[g], dst_ref=dst.at[g], send_sem=a_send.at[which, off], recv_sem=a_recv.at[which, g],
+                    device_id=group_member(groups, g), device_id_type=MESH,
+                ).wait_recv()
+
+    reduce_part(
+        owners, groups, peers, a_arrive, a1_ref, a2_ref, b1_ref, b2_ref, gsum_ref, out_ref, gain_out_ref, *reduce_scratch
+    )
+
     @pl.when(me > 0)
     def _():
         for c in range(CHUNKS):
             chain_copy(c).wait_send()
 
-    for off in range(1, members):
-        g = lax.rem(g_me + members - off, members)
-        for which, dst in ((0, a1_ref), (1, a2_ref)):
-            a_copy(which, dst.at[g_me], dst, off).wait_send()
-            pltpu.make_async_remote_copy(
-                src_ref=dst.at[g], dst_ref=dst.at[g], send_sem=a_send.at[which, off], recv_sem=a_recv.at[which, g],
-                device_id=group_member(groups, g), device_id_type=MESH,
-            ).wait_recv()
-
-
-def reduce_kernel(
-    owners, groups,
+
+def reduce_part(
+    owners, groups, peers, a_arrive,
     a1_ref, a2_ref, b1_ref, b2_ref, gsum_ref,
     out_ref, gain_ref,
-    s1, s2, t1, t2, acc, final, gslot, gquad, *rest,
+    s1, s2, t1, t2, acc, final, gslot, gacc, gland, *rest,
 ):
     me = lax.axis_index("tm")
     vid = lax.axis_index("video")
@@ -222,13 +238,6 @@
     scale = 1.0 / (owners * groups)
     length, rows = a1_ref.shape[1], a2_ref.shape[1]
 
-    barrier = pltpu.get_barrier_semaphore()
-    for off in range(1, members):
-        pl.semaphore_signal(barrier, inc=1, device_id=group_member(groups, lax.rem(g_me + off, members)), device_id_type=MESH)
-    for off in range(1, chips):
-        pl.semaphore_signal(barrier, inc=1, device_id={"tm": lax.rem(me + 2 * off, owners)}, device_id_type=MESH)
-    pl.semaphore_wait(barrier, members - 1 + chips - 1)
-
     def b_copy(which, off):
         g = lax.rem(g_me + off, members)
         v, c = lax.div(g, 2), lax.rem(g, 2)
@@ -252,6 +261,7 @@
     s1[g_me] = b1_ref[core, vid]
     s2[g_me] = b2_ref[core, vid]
     gslot[g_me] = gsum_ref[...]
+    a_arrive()
     for g in range(members):
         t1[:, g * length:(g + 1) * length] = jnp.transpose(a1_ref[g]).astype(BF16)
     for g in range(0, members, 2):
@@ -276,9 +286,8 @@
     for s in range(bits):
         span = features >> (s + 1)
         bit = lax.rem(lax.div(chip, 2 ** s), 2)
-        starts.append((lo + (1 - bit) * span, lo + bit * span, span, chip + (1 - 2 * bit) * 2 ** s))
+        starts.append((lo + (1 - bit) * span, lo + bit * span, span, peers[s]))
         lo = lo + bit * span
-    home = pl.multiple_of(lo, 8)
 
     def r_copy(p, s):
         give, _, span, peer = starts[s]
@@ -286,6 +295,12 @@
             src_ref=acc.at[p, pl.ds(pl.multiple_of(give, 8), span)], dst_ref=lands[s].at[p],
             send_sem=r_send.at[p, s], recv_sem=r_recv.at[p, s],
             device_id={"tm": peer * 2 + core}, device_id_type=MESH,
+        )
+
+    def g_copy(s):
+        return pltpu.make_async_remote_copy(
+            src_ref=gacc.at[s], dst_ref=gland.at[s], send_sem=q_send.at[s], recv_sem=q_recv.at[s],
+            device_id={"tm": peers[s] * 2 + core}, device_id_type=MESH,
         )
 
     def r_finish(p, s):
@@ -318,13 +333,12 @@
         if wave == 0:
             for off in range(1, members):
                 b_arrive(2, off).wait_recv()
-            gquad[chip] = jnp.sum(gslot[...], axis=0)
-            for off in range(1, chips):
-                g_copy = pltpu.make_async_remote_copy(
-                    src_ref=gquad.at[chip], dst_ref=gquad.at[chip], send_sem=q_send.at[off], recv_sem=q_recv.at[chip],
-                    device_id={"tm": lax.rem(me + 2 * off, owners)}, device_id_type=MESH,
-                )
-                g_copy.start()
+            gacc[0] = jnp.sum(gslot[...], axis=0)
+        if 0 < wave <= bits:
+            g_copy(wave - 1).wait_recv()
+            gacc[wave] = gacc[wave - 1] + gland[wave - 1]
+        if wave < bits:
+            g_copy(wave).start()
 
     mine_rows = pl.ds(pl.multiple_of(lo + core * part, 8), part)
     for p in range(pieces):
@@ -337,14 +351,9 @@
         f_copy(p).wait_recv()
         out_ref[2 * which + 1 - core, :, cols] = final[p] * scale
 
-    for off in range(1, chips):
-        src = lax.rem(chip + chips - off, chips)
-        got = pltpu.make_async_remote_copy(
-            src_ref=gquad.at[src], dst_ref=gquad.at[src], send_sem=q_send.at[off], recv_sem=q_recv.at[src],
-            device_id={"tm": lax.rem(me + 2 * off, owners)}, device_id_type=MESH,
-        )
-        got.wait()
-    gain_ref[...] = jnp.sum(gquad[...], axis=0) * scale
+    gain_ref[...] = gacc[bits] * scale
+    for s in range(bits):
+        g_copy(s).wait_send()
     for which in range(3):
         for off in range(1, members):
             b_copy(which, off).wait_send()
@@ -371,19 +380,24 @@
     vmem = pl.BlockSpec(memory_space=pltpu.VMEM)
     smem = pl.BlockSpec(memory_space=pltpu.SMEM)
     sds = jax.ShapeDtypeStruct
-    grad, a1, a2, b1, b2, gsum = pl.pallas_call(
-        functools.partial(chain_kernel, owners, groups, heads),
+    pw = 128 if width % 128 == 0 else width
+    pieces = 2 * (width // pw)
+    dma = pltpu.SemaphoreType.DMA
+    grad, weights, gain = pl.pallas_call(
+        functools.partial(whole_kernel, owners, groups, heads),
         out_shape=(
             sds((rows, features), F32),
-            sds((members, length, features), F32),
-            sds((members, rows, features), F32),
-            sds((2, groups, length, width), F32),
-            sds((2, groups, rows, width), F32),
+            sds((4, features // owners, width), F32),
             sds((1, features), F32),
         ),
         in_specs=[smem] + [vmem] * 9,
-        out_specs=(vmem,) * 6,
+        out_specs=(vmem,) * 3,
         scratch_shapes=[
+            pltpu.VMEM((members, length, features), F32),
+            pltpu.VMEM((members, rows, features), F32),
+            pltpu.VMEM((2, groups, length, width), F32),
+            pltpu.VMEM((2, groups, rows, width), F32),
+            pltpu.VMEM((1, features), F32),
             pltpu.VMEM((rows, features), F32),
             pltpu.VMEM((2, rows, features), F32),
             pltpu.VMEM((rows, heads * length), F32),
@@ -397,26 +411,9 @@
             pltpu.VMEM((rows, features), BF16),
             pltpu.VMEM((rows, features), F32),
             pltpu.VMEM((rows, 128), F32),
-            pltpu.SemaphoreType.DMA((CHUNKS,)),
-            pltpu.SemaphoreType.DMA((CHUNKS,)),
-            pltpu.SemaphoreType.DMA((2, members)),
-            pltpu.SemaphoreType.DMA((2, members)),
-        ],
-        compiler_params=pltpu.CompilerParams(collective_id=0, has_side_effects=True, vmem_limit_bytes=56 * 1024 * 1024),
-        name="chain",
-    )(
-        slot_used[0, 0], memory[0, 0, 0], keyin, mem_cot[0, 0, 0], key_bias[0, 0, 0],
-        norm_gain[None, :], w_query, w_key, w_value, w_out,
-    )
-    pw = 128 if width % 128 == 0 else width
-    pieces = 2 * (width // pw)
-    dma = pltpu.SemaphoreType.DMA
-    weights, gain = pl.pallas_call(
-        functools.partial(reduce_kernel, owners, groups),
-        out_shape=(sds((4, features // owners, width), F32), sds((1, features), F32)),
-        in_specs=[vmem] * 5,
-        out_specs=(vmem,) * 2,
-        scratch_shapes=[
+            pltpu.VMEM((features, features), BF16),
+            pltpu.VMEM((features, features), BF16),
+            dma((CHUNKS,)), dma((CHUNKS,)), dma((2, members)), dma((2, members)),
             pltpu.VMEM((members, length, width), F32),
             pltpu.VMEM((members, rows, width), F32),
             pltpu.VMEM((features, members * length), BF16),
@@ -424,16 +421,20 @@
             pltpu.VMEM((pieces, features, pw), F32),
             pltpu.VMEM((pieces, features // owners, pw), F32),
             pltpu.VMEM((members, 1, features), F32),
-            pltpu.VMEM((chips, 1, features), F32),
+            pltpu.VMEM((bits + 1, 1, features), F32),
+            pltpu.VMEM((max(bits, 1), 1, features), F32),
         ]
         + [pltpu.VMEM((pieces, features >> (s + 1), pw), F32) for s in range(bits)]
         + [
             dma((3, members)), dma((3, members)), dma((pieces, bits)), dma((pieces, bits)),
-            dma((chips,)), dma((chips,)), dma((pieces,)), dma((pieces,)),
+            dma((bits,)), dma((bits,)), dma((pieces,)), dma((pieces,)),
         ],
-        compiler_params=pltpu.CompilerParams(collective_id=1, has_side_effects=True, vmem_limit_bytes=56 * 1024 * 1024),
-        name="reduce",
-    )(a1, a2, b1, b2, gsum)
+        compiler_params=pltpu.CompilerParams(collective_id=0, has_side_effects=True, vmem_limit_bytes=58 * 1024 * 1024),
+        name="whole",
+    )(
+        slot_used[0, 0], memory[0, 0, 0], keyin, mem_cot[0, 0, 0], key_bias[0, 0, 0],
+        norm_gain[None, :], w_query, w_key, w_value, w_out,
+    )
     return (grad[None, None, None], weights[1], weights[2], weights[3], weights[0], gain[0])
 
 

time: 149 us -> 136 us (0.913)
  Pallas kernels: 138 us -> 124 us
    pallas_call x2 -> x1, Pallas kernels: 138 us -> 124 us  [on_device(): pl.pallas_call(functools.partial(whole_kernel, owners, groups, heads), ou...]
where the time goes in v3:
time: 136 us
  Pallas kernels  124 us (91%)
  local copies, waits for them, and re-layouts  5.88 us (4%)
  other arithmetic  3.84 us (3%)
  between operations  1.96 us (1%)
    pallas_call x1, Pallas kernels, on_device(): pl.pallas_call(functools.partial(whole_kernel, owners, groups, heads), ou...  124 us
    unnamed x2, local copies, waits for them, and re-layouts  2.9 us

profile of v3, /device:TPU:0, one launch (start us, length us, event | category | flops | bytes accessed | tf_op | source)
XLA Modules:
  0.0 136.1 jit_solution(4234288468325783997)
XLA Ops:
  2.0 1.3 broadcast_in_dim.8.gain_ref
  3.2 1.3 copy.19
  4.5 0.8 multiply_sine_fusion
  5.3 1.8 %maximum_add_fusion.keyin_ref = f32[128,768]{1,0:T(8,128)} fusion(f32[128,384]{1,0:T(8,128)S(1)} %get-tuple-element.17, f32[128,384]{1,0:T(8,128)S(1)} %get-tuple-element.16, f32[1,1,1,128,768]{4,3,2,1,0:T(8,128)} %param.12), kind=kLoop, calls=%fused_computation | loop fusion | flops 196608 | bytes 1179648 | tf_op jit(solution)/shard_map/add | solution.py:32
  7.1 124.4 %whole.1 = (f32[64,768]{1,0:T(8,128)}, f32[4,48,384]{2,1,0:T(8,128)}, f32[1,768]{1,0:T(1,128)}) custom-call(s32[1]{0:T(128)} %bitcast.18.slot_ref, bf16[64,768]{1,0:T(8,128)(2,1)} %bitcast.21, f32[128,768]{1,0:T(8,128)} %maximum_add_fusion.keyin_ref, bf16[64,768]{1,0:T(8,128)(2,1)} %bitcast.22, f32[12,128]{1,0:T(8,128)} %bitcast.23, ...), custom_call_target="tpu_custom_call" | custom-call | tf_op jit(solution)/shard_map/whole/pallas_call | solution.py:386
  131.5 1.3 reduce
  132.7 1.7 %slice_bitcast_fusion = (f32[48,384]{1,0:T(8,128)}, f32[48,384]{1,0:T(8,128)}, f32[48,384]{1,0:T(8,128)}, f32[48,384]{1,0:T(8,128)}) fusion(f32[4,48,384]{2,1,0:T(8,128)} %get-tuple-element.10), kind=kLoop, calls=%fused_computation.3 | loop fusion | bytes 589824 | tf_op jit(solution)/shard_map/squeeze | solution.py:438
  134.4 1.6 %copy.23 = f32[1,1,1,64,768]{4,3,2,1,0:T(8,128)} copy(f32[1,1,1,64,768]{4,3,2,1,0:T(8,128)} %bitcast.20) | data formatting | bytes 393216
  (2 shorter events, 0.0 us)

commit v4 on v3

--- a/solution.py
+++ b/solution.py
@@ -98,7 +98,8 @@
     normed = (unit * gain_ref[...]).astype(BF16)
     mine[1] = normed.astype(F32)
     keyin = keyin_ref[...].astype(BF16)
-    qp[...] = dot(normed, wq_ref[...], NN).astype(BF16)
+    query = dot(normed, wq_ref[...], NN).astype(BF16)
+    qp[...] = query
     kp = dot(keyin, wk_ref[...], NN).astype(BF16)
     vp = dot(keyin, wv_ref[...], NN).astype(BF16)
     low = lax.broadcasted_iota(jnp.int32, (length, pw), 1) < head
@@ -112,16 +113,19 @@
         vbd[p, length:] = jnp.where(low, zero, vv)
     wot[...] = jnp.transpose(wo_ref[...])
     wqt[...] = jnp.transpose(wq_ref[...])
+    scores = [dot(query[:, p * pw:(p + 1) * pw], kbd[p], NT) for p in range(pairs)]
     for p in range(pairs):
-        s2 = dot(qp[:, p * pw:(p + 1) * pw], kbd[p], NT)
+        halves = []
         for q in range(2):
             h = 2 * p + q
-            s = s2[:, q * length:(q + 1) * length] * scale + bias_ref[h:h + 1, :]
+            s = scores[p][:, q * length:(q + 1) * length] * scale + bias_ref[h:h + 1, :]
             e = jnp.exp(s - jnp.max(s, axis=-1, keepdims=True))
             pr = e / jnp.sum(e, axis=-1, keepdims=True)
             prob[:, h * length:(h + 1) * length] = pr
-            half[:, h * length:(h + 1) * length] = pr.astype(BF16)
-        mine[0, :, p * pw:(p + 1) * pw] = dot(half[:, p * 2 * length:(p + 1) * 2 * length], vbd[p], NN).astype(BF16).astype(F32)
+            halves.append(pr.astype(BF16))
+        both = jnp.concatenate(halves, axis=-1)
+        half[:, p * 2 * length:(p + 1) * 2 * length] = both
+        mine[0, :, p * pw:(p + 1) * pw] = dot(both, vbd[p], NN).astype(BF16).astype(F32)
 
     for off in range(1, members):
         g = lax.rem(g_me + off, members)
@@ -152,19 +156,20 @@
 
         grad_in = incoming[r, :] + cot_ref[r, :].astype(F32)
         og = (live * grad_in).astype(BF16)
-        og_all[r, :] = og
         att = dot(og, wot[...], NN).astype(BF16)
-        att_all[r, :] = att
+        prob_grads = [dot(att[:, p * pw:(p + 1) * pw], vbd[p], NT) for p in range(pairs)]
+        query_grads = []
+        score_grads = []
         for p in range(pairs):
-            pg2 = dot(att[:, p * pw:(p + 1) * pw], vbd[p], NT)
             for q in range(2):
                 h = 2 * p + q
-                pg = pg2[:, q * length:(q + 1) * length]
+                pg = prob_grads[p][:, q * length:(q + 1) * length]
                 pr = prob[r, h * length:(h + 1) * length]
                 inner = jnp.sum(pr * pg, axis=-1, keepdims=True)
-                sg_all[r, h * length:(h + 1) * length] = (pr * (pg - inner) * scale).astype(BF16)
-            qg_all[r, p * pw:(p + 1) * pw] = dot(sg_all[r, p * 2 * length:(p + 1) * 2 * length], kbd[p], NN).astype(BF16)
-        ng = dot(qg_all[r, :], wqt[...], NN)
+                score_grads.append((pr * (pg - inner) * scale).astype(BF16))
+            query_grads.append(dot(jnp.concatenate(score_grads[-2:], axis=-1), kbd[p], NN).astype(BF16))
+        qg = jnp.concatenate(query_grads, axis=-1)
+        ng = dot(qg, wqt[...], NN)
         un = unit_ref[r, :]
         gain_total = gain_total + jnp.sum(ng * un, axis=0, keepdims=True)
         sc = ng * gain_ref[...]
@@ -173,6 +178,12 @@
         @pl.when(me > 0)
         def _():
             chain_copy(c).start()
+
+        og_all[r, :] = og
+        att_all[r, :] = att
+        qg_all[r, :] = qg
+        for h in range(heads):
+            sg_all[r, h * length:(h + 1) * length] = score_grads[h]
 
     gsum_ref[...] = gain_total
 

time: 136 us -> 115 us (0.85)
  Pallas kernels: 124 us -> 103 us
    pallas_call x1, Pallas kernels: 124 us -> 103 us  [on_device(): pl.pallas_call(functools.partial(whole_kernel, owners, groups, heads), ou...]
where the time goes in v4:
time: 115 us
  Pallas kernels  103 us (90%)
  local copies, waits for them, and re-layouts  5.88 us (5%)
  other arithmetic  3.84 us (3%)
  between operations  1.96 us (2%)
    pallas_call x1, Pallas kernels, on_device(): pl.pallas_call(functools.partial(whole_kernel, owners, groups, heads), ou...  103 us
    unnamed x2, local copies, waits for them, and re-layouts  2.9 us

profile of v4, /device:TPU:0, one launch (start us, length us, event | category | flops | bytes accessed | tf_op | source)
XLA Modules:
  0.0 114.6 jit_solution(12295599317226321361)
XLA Ops:
  2.0 1.3 %broadcast_in_dim.8.gain_ref = f32[1,768]{1,0:T(1,128)} reshape(f32[768]{0:T(1024)} %param.17) | data formatting | bytes 6144 | tf_op jit(solution)/shard_map/broadcast_in_dim | solution.py:447
  3.2 1.3 %copy.19 = f32[1,1,1,12,128]{4,3,2,1,0:T(8,128)} copy(f32[1,1,1,12,128]{4,2,3,1,0:T(1,128)} %param.15) | data formatting | bytes 12288
  4.5 0.8 multiply_sine_fusion
  5.3 1.8 %maximum_add_fusion.keyin_ref = f32[128,768]{1,0:T(8,128)} fusion(f32[128,384]{1,0:T(8,128)S(1)} %get-tuple-element.17, f32[128,384]{1,0:T(8,128)S(1)} %get-tuple-element.16, f32[1,1,1,128,768]{4,3,2,1,0:T(8,128)} %param.12), kind=kLoop, calls=%fused_computation | loop fusion | flops 196608 | bytes 1179648 | tf_op jit(solution)/shard_map/add | solution.py:32
  7.1 102.9 %whole.1 = (f32[64,768]{1,0:T(8,128)}, f32[4,48,384]{2,1,0:T(8,128)}, f32[1,768]{1,0:T(1,128)}) custom-call(s32[1]{0:T(128)} %bitcast.18.slot_ref, bf16[64,768]{1,0:T(8,128)(2,1)} %bitcast.21, f32[128,768]{1,0:T(8,128)} %maximum_add_fusion.keyin_ref, bf16[64,768]{1,0:T(8,128)(2,1)} %bitcast.22, f32[12,128]{1,0:T(8,128)} %bitcast.23, ...), custom_call_target="tpu_custom_call" | custom-call | tf_op jit(solution)/shard_map/whole/pallas_call | solution.py:397
  110.0 1.3 %reduce = f32[768]{0:T(1024)} reduce(f32[1,768]{1,0:T(1,128)} %get-tuple-element.11, f32[]{:T(128)} %constant.21), dimensions={0}, to_apply=%get-tuple-element.11.reduce_sub_computation | reduce | bytes 6148 | tf_op jit(solution)/shard_map/whole/pallas_call | solution.py:397
  111.3 1.7 %slice_bitcast_fusion = (f32[48,384]{1,0:T(8,128)}, f32[48,384]{1,0:T(8,128)}, f32[48,384]{1,0:T(8,128)}, f32[48,384]{1,0:T(8,128)}) fusion(f32[4,48,384]{2,1,0:T(8,128)} %get-tuple-element.10), kind=kLoop, calls=%fused_computation.3 | loop fusion | bytes 589824 | tf_op jit(solution)/shard_map/squeeze | solution.py:449
  113.0 1.6 %copy.23 = f32[1,1,1,64,768]{4,3,2,1,0:T(8,128)} copy(f32[1,1,1,64,768]{4,3,2,1,0:T(8,128)} %bitcast.20) | data formatting | bytes 393216
  (2 shorter events, 0.0 us)

commit v5 on v4

--- a/solution.py
+++ b/solution.py
@@ -132,6 +132,26 @@
         a_copy(1, mine.at[lax.rem(g, 2)], a2_ref, off).start()
     a2_ref[g_me] = mine[lax.rem(me, 2)]
 
+    def a_arrive():
+        for off in range(1, members):
+            g = lax.rem(g_me + members - off, members)
+            for which, dst in ((0, a1_ref), (1, a2_ref)):
+                a_copy(which, dst.at[g_me], dst, off).wait_send()
+                pltpu.make_async_remote_copy(
+                    src_ref=dst.at[g], dst_ref=dst.at[g], send_sem=a_send.at[which, off], recv_sem=a_recv.at[which, g],
+                    device_id=group_member(groups, g), device_id_type=MESH,
+                ).wait_recv()
+        t1, t2 = reduce_scratch[2:4]
+        for g in range(members):
+            t1[:, g * length:(g + 1) * length] = jnp.transpose(a1_ref[g]).astype(BF16)
+        for g in range(0, members, 2):
+            both = jnp.concatenate([a2_ref[g], a2_ref[g + 1]], axis=0)
+            t2[:, g * rows:(g + 2) * rows] = jnp.transpose(both).astype(BF16)
+
+    @pl.when(me < owners // 4)
+    def _():
+        a_arrive()
+
     live = slot_ref[0].astype(F32)
     step = rows // CHUNKS
 
@@ -198,27 +218,20 @@
                 out[which, v, :, lo - v * width:hi - v * width] = value[:, lo - p * pw:hi - p * pw]
 
     for p in range(pairs):
-        for which, (left_ref, right_ref) in enumerate(((sg_all, qp), (half, att_all))):
-            right = right_ref[:, p * pw:(p + 1) * pw]
-            right = jnp.concatenate([jnp.where(lowr, right, zr), jnp.where(lowr, zr, right)], axis=0)
-            base = 2 * p * length
-            left = jnp.concatenate([left_ref[:, base:base + length], left_ref[:, base + length:base + 2 * length]], axis=0)
-            put(b1_ref, which, p, dot(left, right, TN).astype(BF16).astype(F32))
         put(b2_ref, 0, p, og_all[:, p * pw:(p + 1) * pw].astype(F32))
         put(b2_ref, 1, p, qg_all[:, p * pw:(p + 1) * pw].astype(F32))
 
-    def a_arrive():
-        for off in range(1, members):
-            g = lax.rem(g_me + members - off, members)
-            for which, dst in ((0, a1_ref), (1, a2_ref)):
-                a_copy(which, dst.at[g_me], dst, off).wait_send()
-                pltpu.make_async_remote_copy(
-                    src_ref=dst.at[g], dst_ref=dst.at[g], send_sem=a_send.at[which, off], recv_sem=a_recv.at[which, g],
-                    device_id=group_member(groups, g), device_id_type=MESH,
-                ).wait_recv()
+    def token_grads():
+        for p in range(pairs):
+            for which, (left_ref, right_ref) in enumerate(((sg_all, qp), (half, att_all))):
+                right = right_ref[:, p * pw:(p + 1) * pw]
+                right = jnp.concatenate([jnp.where(lowr, right, zr), jnp.where(lowr, zr, right)], axis=0)
+                base = 2 * p * length
+                left = jnp.concatenate([left_ref[:, base:base + length], left_ref[:, base + length:base + 2 * length]], axis=0)
+                put(b1_ref, which, p, dot(left, right, TN).astype(BF16).astype(F32))
 
     reduce_part(
-        owners, groups, peers, a_arrive, a1_ref, a2_ref, b1_ref, b2_ref, gsum_ref, out_ref, gain_out_ref, *reduce_scratch
+        owners, groups, peers, token_grads, a_arrive, b1_ref, b2_ref, gsum_ref, out_ref, gain_out_ref, *reduce_scratch
     )
 
     @pl.when(me > 0)
@@ -228,8 +241,8 @@
 
 
 def reduce_part(
-    owners, groups, peers, a_arrive,
-    a1_ref, a2_ref, b1_ref, b2_ref, gsum_ref,
+    owners, groups, peers, token_grads, a_arrive,
+    b1_ref, b2_ref, gsum_ref,
     out_ref, gain_ref,
     s1, s2, t1, t2, acc, final, gslot, gacc, gland, *rest,
 ):
@@ -247,7 +260,6 @@
     block = features // chips
     part = block // 2
     scale = 1.0 / (owners * groups)
-    length, rows = a1_ref.shape[1], a2_ref.shape[1]
 
     def b_copy(which, off):
         g = lax.rem(g_me + off, members)
@@ -266,20 +278,23 @@
             device_id=group_member(groups, g), device_id_type=MESH,
         )
 
-    for which in (2, 1, 0):
+    for which in (2, 1):
         for off in range(1, members):
             b_copy(which, off).start()
+    token_grads()
+    for off in range(1, members):
+        b_copy(0, off).start()
     s1[g_me] = b1_ref[core, vid]
     s2[g_me] = b2_ref[core, vid]
     gslot[g_me] = gsum_ref[...]
-    a_arrive()
-    for g in range(members):
-        t1[:, g * length:(g + 1) * length] = jnp.transpose(a1_ref[g]).astype(BF16)
-    for g in range(0, members, 2):
-        both = jnp.concatenate([a2_ref[g], a2_ref[g + 1]], axis=0)
-        t2[:, g * rows:(g + 2) * rows] = jnp.transpose(both).astype(BF16)
-
-    order = [int(format(i, "b").zfill(bits)[::-1], 2) if bits else 0 for i in range(chips)]
+
+    @pl.when(me >= owners // 4)
+    def _():
+        a_arrive()
+
+    plain = list(range(bits))
+    swapped = plain[1::-1] + plain[2:]
+    sequence = [swapped if per > 1 and bits > 1 and p % per == 0 else plain for p in range(pieces)]
 
     def products(which):
         slots, left = ((s2, t2), (s1, t1))[which]
@@ -289,19 +304,22 @@
             right = slots[:, :, i * pw:(i + 1) * pw].reshape(left.shape[1], pw).astype(BF16)
             value = dot(left[...], right, NN)
             for pos in range(chips):
-                k = order[pos]
+                k = sum(((pos >> (bits - 1 - n)) & 1) << bit for n, bit in enumerate(sequence[which * per + i]))
                 acc[which * per + i, pos * block:(pos + 1) * block, :] = value[k * block:(k + 1) * block, :]
 
-    starts = []
-    lo = 0
-    for s in range(bits):
-        span = features >> (s + 1)
-        bit = lax.rem(lax.div(chip, 2 ** s), 2)
-        starts.append((lo + (1 - bit) * span, lo + bit * span, span, peers[s]))
-        lo = lo + bit * span
+    starts, home = [], []
+    for p in range(pieces):
+        stages, lo = [], 0
+        for n, b in enumerate(sequence[p]):
+            span = features >> (n + 1)
+            bit = lax.rem(lax.div(chip, 2 ** b), 2)
+            stages.append((lo + (1 - bit) * span, lo + bit * span, span, peers[b]))
+            lo = lo + bit * span
+        starts.append(stages)
+        home.append(lo)
 
     def r_copy(p, s):
-        give, _, span, peer = starts[s]
+        give, _, span, peer = starts[p][s]
         return pltpu.make_async_remote_copy(
             src_ref=acc.at[p, pl.ds(pl.multiple_of(give, 8), span)], dst_ref=lands[s].at[p],
             send_sem=r_send.at[p, s], recv_sem=r_recv.at[p, s],
@@ -315,28 +333,28 @@
         )
 
     def r_finish(p, s):
-        _, keep, span, _ = starts[s]
+        _, keep, span, _ = starts[p][s]
         r_copy(p, s).wait_recv()
         at = pl.ds(pl.multiple_of(keep, 8), span)
         acc[p, at, :] = acc[p, at, :] + lands[s][p]
 
     def f_copy(p):
-        theirs = pl.ds(pl.multiple_of(lo + (1 - core) * part, 8), part)
+        theirs = pl.ds(pl.multiple_of(home[p] + (1 - core) * part, 8), part)
         return pltpu.make_async_remote_copy(
             src_ref=acc.at[p, theirs], dst_ref=final.at[p], send_sem=f_send.at[p], recv_sem=f_recv.at[p],
             device_id={"tm": chip * 2 + 1 - core}, device_id_type=MESH,
         )
 
+    for which in range(2):
+        products(which)
+        for p in range(which * per, (which + 1) * per):
+            r_copy(p, 0).start()
+
     for wave in range(pieces + bits):
-        if wave == 0:
-            products(0)
-        if wave == per:
-            products(1)
-        for s in reversed(range(bits + 1)):
-            p = wave - s
+        for s in reversed(range(1, bits + 1)):
+            p = wave + 1 - s
             if 0 <= p < pieces:
-                if s > 0:
-                    r_finish(p, s - 1)
+                r_finish(p, s - 1)
                 if s < bits:
                     r_copy(p, s).start()
                 else:
@@ -351,10 +369,10 @@
         if wave < bits:
             g_copy(wave).start()
 
-    mine_rows = pl.ds(pl.multiple_of(lo + core * part, 8), part)
     for p in range(pieces):
         which, i = p // per, p % per
         cols = slice(i * pw, (i + 1) * pw)
+        mine_rows = pl.ds(pl.multiple_of(home[p] + core * part, 8), part)
         out_ref[2 * which + core, :, cols] = acc[p, mine_rows, :] * scale
     for p in range(pieces):
         which, i = p // per, p % per

time: 115 us -> 120 us (1.043)
  Pallas kernels: 103 us -> 108 us
    pallas_call x1, Pallas kernels: 103 us -> 108 us  [on_device(): pl.pallas_call(functools.partial(whole_kernel, owners, groups, heads), ou...]
where the time goes in v5:
time: 120 us
  Pallas kernels  108 us (90%)
  local copies, waits for them, and re-layouts  5.88 us (5%)
  other arithmetic  3.84 us (3%)
  between operations  1.96 us (2%)
    pallas_call x1, Pallas kernels, on_device(): pl.pallas_call(functools.partial(whole_kernel, owners, groups, heads), ou...  108 us
    unnamed x2, local copies, waits for them, and re-layouts  2.9 us

profile of v5, /device:TPU:0, one launch (start us, length us, event | category | flops | bytes accessed | tf_op | source)
XLA Modules:
  0.0 119.9 jit_solution(4531286533640631075)
XLA Ops:
  2.0 1.3 %broadcast_in_dim.8.gain_ref = f32[1,768]{1,0:T(1,128)} reshape(f32[768]{0:T(1024)} %param.17) | data formatting | bytes 6144 | tf_op jit(solution)/shard_map/broadcast_in_dim | solution.py:465
  3.2 1.3 %copy.19 = f32[1,1,1,12,128]{4,3,2,1,0:T(8,128)} copy(f32[1,1,1,12,128]{4,2,3,1,0:T(1,128)} %param.15) | data formatting | bytes 12288
  4.5 0.8 multiply_sine_fusion
  5.3 1.8 %maximum_add_fusion.keyin_ref = f32[128,768]{1,0:T(8,128)} fusion(f32[128,384]{1,0:T(8,128)S(1)} %get-tuple-element.17, f32[128,384]{1,0:T(8,128)S(1)} %get-tuple-element.16, f32[1,1,1,128,768]{4,3,2,1,0:T(8,128)} %param.12), kind=kLoop, calls=%fused_computation | loop fusion | flops 196608 | bytes 1179648 | tf_op jit(solution)/shard_map/add | solution.py:32
  7.1 108.2 %whole.1 = (f32[64,768]{1,0:T(8,128)}, f32[4,48,384]{2,1,0:T(8,128)}, f32[1,768]{1,0:T(1,128)}) custom-call(s32[1]{0:T(128)} %bitcast.18.slot_ref, bf16[64,768]{1,0:T(8,128)(2,1)} %bitcast.21, f32[128,768]{1,0:T(8,128)} %maximum_add_fusion.keyin_ref, bf16[64,768]{1,0:T(8,128)(2,1)} %bitcast.22, f32[12,128]{1,0:T(8,128)} %bitcast.23, ...), custom_call_target="tpu_custom_call" | custom-call | tf_op jit(solution)/shard_map/whole/pallas_call | solution.py:415
  115.3 1.3 %reduce = f32[768]{0:T(1024)} reduce(f32[1,768]{1,0:T(1,128)} %get-tuple-element.11, f32[]{:T(128)} %constant.21), dimensions={0}, to_apply=%get-tuple-element.11.reduce_sub_computation | reduce | bytes 6148 | tf_op jit(solution)/shard_map/whole/pallas_call | solution.py:415
  116.5 1.7 %slice_bitcast_fusion = (f32[48,384]{1,0:T(8,128)}, f32[48,384]{1,0:T(8,128)}, f32[48,384]{1,0:T(8,128)}, f32[48,384]{1,0:T(8,128)}) fusion(f32[4,48,384]{2,1,0:T(8,128)} %get-tuple-element.10), kind=kLoop, calls=%fused_computation.3 | loop fusion | bytes 589824 | tf_op jit(solution)/shard_map/squeeze | solution.py:467
  118.2 1.6 %copy.23 = f32[1,1,1,64,768]{4,3,2,1,0:T(8,128)} copy(f32[1,1,1,64,768]{4,3,2,1,0:T(8,128)} %bitcast.20) | data formatting | bytes 393216
  (2 shorter events, 0.0 us)
